TPU v7x, 128 devices: a whole 4x4x4 slice. The times are simulated.
128 devices in a mesh: tok: 16 (over x_hi, z, core), wid: 8 (over y, x_lo).
Axes of the slice: x: 4 (x_hi: 2, x_lo: 2; x = x_hi * 2 + x_lo), y: 4, z: 4, core: 2. Of those that a mesh axis runs over, the one named last changes fastest.
Arguments:
- tokens: bfloat16 [9344, 1024], P('tok', 'wid'), may hold values from -6 to 6
- image_ids: int32 [9344], P('tok'), may hold values from 1 to 9360, as said below
- norm_gains: float32 [2, 2, 1024], P(None, None, 'wid'), may hold values from 0.5 to 1.5
- norm_shifts: float32 [2, 2, 1024], P(None, None, 'wid'), may hold values from -1.8 to 1.8
- qkv_weight: bfloat16 [2, 1024, 3, 1024], P(None, 'tok', None, 'wid'), may hold values from -0.1875 to 0.1875
- qv_bias: float32 [2, 2, 1024], P(None, None, 'wid'), may hold values from -3 to 3
- out_weight: bfloat16 [2, 1024, 1024], P(None, 'wid', 'tok'), may hold values from -0.75 to 0.75
- out_bias: float32 [2, 1024], P(None, 'wid'), may hold values from -3 to 3
- up_weight: bfloat16 [2, 1024, 4096], P(None, 'tok', 'wid'), may hold values from -0.1875 to 0.1875
- up_bias: float32 [2, 4096], P(None, 'wid'), may hold values from -3 to 3
- down_weight: bfloat16 [2, 4096, 1024], P(None, 'wid', 'tok'), may hold values from -0.125 to 0.125
- down_bias: float32 [2, 1024], P(None, 'wid'), may hold values from -3 to 3
- out_grad: bfloat16 [9344, 1024], P('tok', 'wid'), may hold values from -6 to 6
Outputs:
- activations: bfloat16 [9344, 1024], P('tok', 'wid')
- input_grad: float32 [9344, 1024], P('tok', 'wid')
- gain_grad: float32 [2, 2, 1024], P(None, None, 'wid')
- shift_grad: float32 [2, 2, 1024], P(None, None, 'wid')
- qkv_grad: float32 [2, 1024, 3, 1024], P(None, 'tok', None, 'wid')
- qv_bias_grad: float32 [2, 2, 1024], P(None, None, 'wid')
- out_weight_grad: float32 [2, 1024, 1024], P(None, 'wid', 'tok')
- out_bias_grad: float32 [2, 1024], P(None, 'wid')
- up_weight_grad: float32 [2, 1024, 4096], P(None, 'tok', 'wid')
- up_bias_grad: float32 [2, 4096], P(None, 'wid')
- down_weight_grad: float32 [2, 4096, 1024], P(None, 'wid', 'tok')
- down_bias_grad: float32 [2, 1024], P(None, 'wid')
Inputs may be any that keep to these rules, and one draw needn't show every extreme that they name: `image_ids`: images 1 to 16, in order, each hold exactly 577 consecutive tokens; each aligned block of 584 tokens holds one whole image; every other token has a number of its own above 16, and the last token of each block is such a token.
All inputs are finite; a program needn't handle non-finite values.
Results may differ from a plain program's by a relative error of at most 0.02.
Values may be sent and summed in bfloat16 or wider, within the bound.
No kernel may reach another device: no remote copies, remote signals or barrier semaphores. Data moves between devices by JAX's collectives and lax.ppermute only.
A program may use at most 128 MiB of HBM per device.

v0:
```python
import jax
import jax.numpy as jnp
from jax import lax
from jax.sharding import PartitionSpec as P

HEAD = 64
LAYERS = 2


EPSILON = 1e-06


def copy_for_each(value, axis):
    copies = jnp.broadcast_to(value, (lax.axis_size(axis), *value.shape))
    return lax.all_to_all(copies, axis, split_axis=0, concat_axis=0, tiled=True)


def over_copies(value, axis):
    everything = copy_for_each(value, axis)
    return jnp.sum(everything, axis=0)


def in_one(arrays, axis):
    line, at, finished = (jnp.concatenate([a.reshape(-1) for a in arrays]), 0, [])
    so_far = over_copies(line, axis)
    for a in arrays:
        finished.append(so_far[at : at + a.size].reshape(a.shape))
        at += a.size
    return tuple(finished)


def in_order(tiles, dim):
    dims = list(tiles.shape[1:])
    dims[dim] *= tiles.shape[0]
    return jnp.moveaxis(tiles, 0, dim).reshape(dims)


def collect(value, axis, dim):
    tiles = copy_for_each(value, axis)
    return in_order(tiles, dim)


def cut_along(value, dim, peers):
    before, after = (value.shape[:dim], value.shape[dim + 1 :])
    return jnp.moveaxis(value.reshape(*before, peers, -1, *after), dim, 0)


def summed_on_arrival(value, axis, dim):
    tiles = cut_along(value, dim, lax.axis_size(axis))
    arrived = lax.all_to_all(tiles, axis, split_axis=0, concat_axis=0, tiled=True)
    return arrived.astype(jnp.float32).sum(axis=0)


def turned_gather(arrays, axis, dims):
    turned = [jnp.moveaxis(a, dim, 0) for a, dim in zip(arrays, dims)]
    both = jnp.concatenate([t.reshape(len(t), -1) for t in turned], axis=1)
    filled, at, finished = (lax.all_gather(both, axis, axis=0, tiled=True), 0, [])
    for t, dim in zip(turned, dims):
        piece = filled[:, at : at + t[0].size].reshape(-1, *t.shape[1:])
        finished.append(jnp.moveaxis(piece, 0, dim))
        at += t[0].size
    return tuple(finished)


def sum_together(arrays, axis, dims):
    peers = lax.axis_size(axis)
    tiles = [cut_along(a, dim, peers) for a, dim in zip(arrays, dims)]
    lines = jnp.concatenate([b.reshape(peers, -1) for b in tiles], axis=1)
    span = max(16, -(-lines.shape[1] // 1024) * 8)
    lines = jnp.pad(lines, ((0, 0), (0, span * 128 - lines.shape[1]))).reshape(-1, 128)
    line, at, finished = (lax.psum_scatter(lines, axis, tiled=True).reshape(-1), 0, [])
    for b in tiles:
        part = b[0]
        finished.append(line[at : at + part.size].reshape(part.shape))
        at += part.size
    return tuple(finished)


def contract_rows(left, right):
    return lax.dot_general(
        left, right, (((0,), (0,)), ((), ())), preferred_element_type=jnp.float32
    )


def contract_cols(left, right):
    return lax.dot_general(
        left, right, (((1,), (1,)), ((), ())), preferred_element_type=jnp.float32
    )


def norm_forward(values, gain, shift, width):
    totals = in_one((jnp.sum(values, axis=1), jnp.sum(values * values, axis=1)), "wid")
    mean = totals[0] / width
    spread = totals[1] / width - mean * mean
    row_scale = lax.rsqrt(spread + EPSILON)
    centred = (values - mean[:, None]) * row_scale[:, None]
    return (centred, row_scale, centred * gain + shift)


def norm_backward(dnormed, centred, row_scale, gain, width):
    scaled = dnormed * gain
    totals = in_one((jnp.sum(scaled, axis=1), jnp.sum(scaled * centred, axis=1)), "wid")
    dvalues = row_scale[:, None] * (
        scaled - totals[0][:, None] / width - centred * (totals[1][:, None] / width)
    )
    return (dvalues, jnp.sum(dnormed * centred, axis=0), jnp.sum(dnormed, axis=0))


def full_rows(values):
    return collect(values, "wid", 1)


def width_sum(partial_value):
    return summed_on_arrival(partial_value.astype(jnp.bfloat16), "wid", 1)


def split_heads(values, heads):
    return values.reshape(values.shape[0], heads, values.shape[1] // heads)


def scores_of(query, keys, token_ids, heads):
    raw = jnp.einsum(
        "qhe,khe->hqk",
        split_heads(query, heads),
        split_heads(keys, heads),
        preferred_element_type=jnp.float32,
    )
    allowed = token_ids[:, None] == token_ids[None, :]
    return jnp.where(allowed[None], raw * HEAD ** (-0.5), -1e30)


def attend(query, keys, values, token_ids, heads):
    scores = scores_of(query, keys, token_ids, heads)
    top = jnp.max(scores, axis=2, keepdims=True)
    expo = jnp.exp(scores - top)
    total = jnp.sum(expo, axis=2, keepdims=True)
    probs = (expo / total).astype(jnp.bfloat16)
    mixed = jnp.einsum(
        "hqk,khe->qhe", probs, split_heads(values, heads), preferred_element_type=jnp.float32
    )
    return (mixed.reshape(query.shape[0], query.shape[1]), top + jnp.log(total))


def attend_back(dmixed, query, keys, values, token_ids, logsum, heads):
    scores = scores_of(query, keys, token_ids, heads)
    probs = jnp.exp(scores - logsum)
    dmix3 = split_heads(dmixed, heads)
    dvalues = jnp.einsum(
        "hqk,qhe->khe", probs.astype(jnp.bfloat16), dmix3, preferred_element_type=jnp.float32
    )
    dprobs = jnp.einsum(
        "qhe,khe->hqk", dmix3, split_heads(values, heads), preferred_element_type=jnp.float32
    )
    centre = jnp.sum(probs * dprobs, axis=2, keepdims=True)
    dscores = (probs * (dprobs - centre)).astype(jnp.bfloat16)
    scale = HEAD ** (-0.5)
    dquery = (
        jnp.einsum(
            "hqk,khe->qhe", dscores, split_heads(keys, heads), preferred_element_type=jnp.float32
        )
        * scale
    )
    dkeys = (
        jnp.einsum(
            "hqk,qhe->khe", dscores, split_heads(query, heads), preferred_element_type=jnp.float32
        )
        * scale
    )
    rows = query.shape[0]
    return (dquery.reshape(rows, -1), dkeys.reshape(rows, -1), dvalues.reshape(rows, -1))


def gelu_slope(pre):
    return (
        0.5 * (1.0 + lax.erf(pre * 0.7071067811865476))
        + pre * jnp.exp(-0.5 * pre * pre) * 0.3989422804014327
    )


def shards(
    tokens,
    image_ids,
    norm_gains,
    norm_shifts,
    qkv_weight,
    qv_bias,
    out_weight,
    out_bias,
    up_weight,
    up_bias,
    down_weight,
    down_bias,
    out_grad,
):
    rows = tokens.shape[0]
    cols = tokens.shape[1]
    width = cols * lax.axis_size("wid")
    heads = cols // HEAD
    state = tokens.astype(jnp.float32)
    kept = []
    saved = []
    for layer in range(LAYERS):
        matrices = turned_gather(
            (qkv_weight[layer], out_weight[layer], up_weight[layer], down_weight[layer]),
            "tok",
            (0, 1, 0, 1),
        )
        qkv_full, out_full, up_full, down_full = matrices
        kept.append(matrices)
        centred1, scale1, normed1 = norm_forward(
            state, norm_gains[layer, 0], norm_shifts[layer, 0], width
        )
        rows1 = full_rows(normed1.astype(jnp.bfloat16))
        proj = jnp.dot(
            rows1, qkv_full.reshape(width, 3 * cols), preferred_element_type=jnp.float32
        ).reshape(rows, 3, cols)
        query = (proj[:, 0] + qv_bias[layer, 0]).astype(jnp.bfloat16)
        keys = proj[:, 1].astype(jnp.bfloat16)
        values = (proj[:, 2] + qv_bias[layer, 1]).astype(jnp.bfloat16)
        mixed, logsum = attend(query, keys, values, image_ids, heads)
        attended = mixed.astype(jnp.bfloat16)
        branch = width_sum(jnp.dot(attended, out_full, preferred_element_type=jnp.float32))
        middle = state + branch + out_bias[layer]
        centred2, scale2, normed2 = norm_forward(
            middle, norm_gains[layer, 1], norm_shifts[layer, 1], width
        )
        rows2 = full_rows(normed2.astype(jnp.bfloat16))
        pre = jnp.dot(rows2, up_full, preferred_element_type=jnp.float32) + up_bias[layer]
        hidden = jax.nn.gelu(pre, approximate=False).astype(jnp.bfloat16)
        state = (
            middle
            + width_sum(jnp.dot(hidden, down_full, preferred_element_type=jnp.float32))
            + down_bias[layer]
        )
        saved.append(
            (
                centred1,
                scale1,
                rows1,
                query,
                keys,
                values,
                logsum,
                attended,
                centred2,
                scale2,
                rows2,
                pre,
                hidden,
            )
        )
    activations = state.astype(jnp.bfloat16)
    grad_state = out_grad.astype(jnp.float32)
    results = []
    for layer in reversed(range(LAYERS)):
        matrices = turned_gather(
            (qkv_weight[layer], out_weight[layer], up_weight[layer], down_weight[layer]),
            "tok",
            (0, 1, 0, 1),
        )
        qkv_full, out_full, up_full, down_full = matrices
        (
            centred1,
            scale1,
            rows1,
            query,
            keys,
            values,
            logsum,
            attended,
            centred2,
            scale2,
            rows2,
            pre,
            hidden,
        ) = saved[layer]
        grad_branch = grad_state.astype(jnp.bfloat16)
        grad_rows = full_rows(grad_branch)
        dhidden = contract_cols(grad_rows, down_full)
        ddown = contract_rows(hidden, grad_rows)
        dpre = (dhidden * gelu_slope(pre)).astype(jnp.bfloat16)
        dup = contract_rows(rows2, dpre)
        dnormed2 = width_sum(contract_cols(dpre, up_full))
        dmiddle, dgain2, dshift2 = norm_backward(
            dnormed2, centred2, scale2, norm_gains[layer, 1], width
        )
        grad_middle = grad_state + dmiddle
        grad_attn = grad_middle.astype(jnp.bfloat16)
        attn_rows = full_rows(grad_attn)
        dmixed = contract_cols(attn_rows, out_full).astype(jnp.bfloat16)
        dout = contract_rows(attended, attn_rows)
        dquery, dkeys, dvalues = attend_back(dmixed, query, keys, values, image_ids, logsum, heads)
        dquery = dquery.astype(jnp.bfloat16)
        dkeys = dkeys.astype(jnp.bfloat16)
        dvalues = dvalues.astype(jnp.bfloat16)
        dproj = jnp.stack([dquery, dkeys, dvalues], axis=1).reshape(rows, 3 * cols)
        dqkv = contract_rows(rows1, dproj).reshape(width, 3, cols)
        dnormed1 = width_sum(contract_cols(dproj, qkv_full.reshape(width, 3 * cols)))
        dinput, dgain1, dshift1 = norm_backward(
            dnormed1, centred1, scale1, norm_gains[layer, 0], width
        )
        grad_state = grad_middle + dinput
        weight_parts = tuple(
            (
                part.astype(jnp.float32)
                for part in sum_together(
                    (
                        dqkv.astype(jnp.bfloat16),
                        dout.astype(jnp.bfloat16),
                        dup.astype(jnp.bfloat16),
                        ddown.astype(jnp.bfloat16),
                    ),
                    "tok",
                    (0, 1, 0, 1),
                )
            )
        )
        vector_parts = in_one(
            (
                jnp.stack([dgain1, dgain2]),
                jnp.stack([dshift1, dshift2]),
                jnp.stack(
                    [
                        jnp.sum(dquery, axis=0, dtype=jnp.float32),
                        jnp.sum(dvalues, axis=0, dtype=jnp.float32),
                    ]
                ),
                jnp.sum(grad_attn, axis=0, dtype=jnp.float32),
                jnp.sum(dpre, axis=0, dtype=jnp.float32),
                jnp.sum(grad_branch, axis=0, dtype=jnp.float32),
            ),
            "tok",
        )
        results.append((weight_parts, vector_parts))
    results = results[::-1]
    gain_grad = jnp.stack([item[1][0] for item in results])
    shift_grad = jnp.stack([item[1][1] for item in results])
    qkv_grad = jnp.stack([item[0][0] for item in results])
    qv_bias_grad = jnp.stack([item[1][2] for item in results])
    out_weight_grad = jnp.stack([item[0][1] for item in results])
    out_bias_grad = jnp.stack([item[1][3] for item in results])
    up_weight_grad = jnp.stack([item[0][2] for item in results])
    up_bias_grad = jnp.stack([item[1][4] for item in results])
    down_weight_grad = jnp.stack([item[0][3] for item in results])
    down_bias_grad = jnp.stack([item[1][5] for item in results])
    return (
        activations,
        grad_state,
        gain_grad,
        shift_grad,
        qkv_grad,
        qv_bias_grad,
        out_weight_grad,
        out_bias_grad,
        up_weight_grad,
        up_bias_grad,
        down_weight_grad,
        down_bias_grad,
    )


def solution(mesh):
    placed = (
        P("tok", "wid"),
        P("tok"),
        P(None, None, "wid"),
        P(None, None, "wid"),
        P(None, "tok", None, "wid"),
        P(None, None, "wid"),
        P(None, "wid", "tok"),
        P(None, "wid"),
        P(None, "tok", "wid"),
        P(None, "wid"),
        P(None, "wid", "tok"),
        P(None, "wid"),
        P("tok", "wid"),
    )
    return jax.shard_map(
        shards,
        mesh=mesh,
        in_specs=placed,
        out_specs=(
            P("tok", "wid"),
            P("tok", "wid"),
            P(None, None, "wid"),
            P(None, None, "wid"),
            P(None, "tok", None, "wid"),
            P(None, None, "wid"),
            P(None, "wid", "tok"),
            P(None, "wid"),
            P(None, "tok", "wid"),
            P(None, "wid"),
            P(None, "wid", "tok"),
            P(None, "wid"),
        ),
        check_vma=False,
    )
```

profile of v0, /device:TPU:0, one launch (start us, length us, event | category | flops | bytes accessed | tf_op | source)
XLA Modules:
  0.0 663.4 jit_solution(15200785847453675437)
XLA Ops:
  12.4 5.5 all-to-all-start
  18.4 5.7 all-to-all-done
  25.7 3.7 all-to-all-start.1
  31.2 14.3 %all-to-all-done.1 = bf16[8,584,128]{2,1,0:T(8,128)(2,1)S(1)} async-done(((bf16[8,584,128]{2,1,0:T(8,128)(2,1)}), bf16[8,584,128]{2,1,0:T(8,128)(2,1)S(1)}, u32[]{:S(2)}, u32[]{:S(2)}) %all-to-all-start.1) | async-done | bytes 1196064 | tf_op jit(solution)/shard_map/all_to_all | solution.py:15
  47.1 17.8 %all-gather.3.cloned.1.call-done = bf16[1024,1536]{1,0:T(8,128)(2,1)} async-done(((bf16[64,1536]{1,0:T(8,128)(2,1)}), bf16[1024,1536]{1,0:T(8,128)(2,1)}) %all-gather.3.cloned.1.call-update) | async-done | bytes 3145744 | tf_op jit(solution)/shard_map/all_gather | solution.py:57
  75.7 4.4 all-to-all-start.2
  81.5 16.7 %all-to-all-done.2 = bf16[8,584,128]{2,1,0:T(8,128)(2,1)} async-done(((bf16[8,584,128]{2,1,0:T(8,128)(2,1)}), bf16[8,584,128]{2,1,0:T(8,128)(2,1)}, u32[]{:S(2)}, u32[]{:S(2)}) %all-to-all-start.2) | async-done | bytes 1196064 | tf_op jit(solution)/shard_map/all_to_all | solution.py:50
  100.0 8.8 %all_to_all.140 = f32[8,1,1168]{2,1,0:T(1,128)S(1)} all-to-all(f32[8,1,1168]{2,1,0:T(1,128)S(1)} %broadcast_in_dim.120), channel_id=1, replica_groups=mesh['tok'=16,'wid'=8] {'wid'}, dimensions={0} | all-to-all | bytes 74752 | tf_op jit(solution)/shard_map/all_to_all | solution.py:15
  110.4 4.4 all-to-all-start.4
  115.3 24.1 %all-to-all-done.4 = bf16[8,584,128]{2,1,0:T(8,128)(2,1)} async-done(((bf16[8,584,128]{2,1,0:T(8,128)(2,1)}), bf16[8,584,128]{2,1,0:T(8,128)(2,1)}, u32[]{:S(2)}, u32[]{:S(2)}) %all-to-all-start.4) | async-done | bytes 1196064 | tf_op jit(solution)/shard_map/all_to_all | solution.py:15
  139.5 5.8 fusion.25
  148.8 4.9 all-to-all-start.5
  154.2 15.8 %all-to-all-done.5 = bf16[8,584,128]{2,1,0:T(8,128)(2,1)} async-done(((bf16[8,584,128]{2,1,0:T(8,128)(2,1)}), bf16[8,584,128]{2,1,0:T(8,128)(2,1)}, u32[]{:S(2)}, u32[]{:S(2)}) %all-to-all-start.5) | async-done | bytes 1196064 | tf_op jit(solution)/shard_map/all_to_all | solution.py:50
  172.5 8.8 %all_to_all.141 = f32[8,1,1168]{2,1,0:T(1,128)S(1)} all-to-all(f32[8,1,1168]{2,1,0:T(1,128)S(1)} %broadcast_in_dim.122), channel_id=1, replica_groups=mesh['tok'=16,'wid'=8] {'wid'}, dimensions={0} | all-to-all | bytes 74752 | tf_op jit(solution)/shard_map/all_to_all | solution.py:15
  183.8 4.4 all-to-all-start.7
  192.8 10.9 %all-to-all-done.7 = bf16[8,584,128]{2,1,0:T(8,128)(2,1)} async-done(((bf16[8,584,128]{2,1,0:T(8,128)(2,1)}), bf16[8,584,128]{2,1,0:T(8,128)(2,1)}, u32[]{:S(2)}, u32[]{:S(2)}) %all-to-all-start.7) | async-done | bytes 1196064 | tf_op jit(solution)/shard_map/all_to_all | solution.py:15
  225.3 17.7 %all_to_all.142 = bf16[8,584,128]{2,1,0:T(8,128)(2,1)S(1)} all-to-all(bf16[8,584,128]{2,1,0:T(8,128)(2,1)S(1)} %bitcast.374), channel_id=1, replica_groups=mesh['tok'=16,'wid'=8] {'wid'}, dimensions={0} | all-to-all | bytes 2392064 | tf_op jit(solution)/shard_map/all_to_all | solution.py:50
  245.0 8.7 %all_to_all.143 = f32[8,1,1168]{2,1,0:T(1,128)S(1)} all-to-all(f32[8,1,1168]{2,1,0:T(1,128)S(1)} %broadcast_in_dim.124), channel_id=1, replica_groups=mesh['tok'=16,'wid'=8] {'wid'}, dimensions={0} | all-to-all | bytes 74752 | tf_op jit(solution)/shard_map/all_to_all | solution.py:15
  255.2 16.3 %all_to_all.144 = bf16[8,584,128]{2,1,0:T(8,128)(2,1)} all-to-all(bf16[8,584,128]{2,1,0:T(8,128)(2,1)S(1)} %broadcast_in_dim.125), channel_id=1, replica_groups=mesh['tok'=16,'wid'=8] {'wid'}, dimensions={0} | all-to-all | bytes 2392064 | tf_op jit(solution)/shard_map/all_to_all | solution.py:15
  272.7 4.6 all-to-all-start.12
  277.3 6.0 fusion.28
  283.3 6.8 %all-to-all-done.12 = bf16[8,584,128]{2,1,0:T(8,128)(2,1)} async-done(((bf16[8,584,128]{2,1,0:T(8,128)(2,1)}), bf16[8,584,128]{2,1,0:T(8,128)(2,1)}, u32[]{:S(2)}, u32[]{:S(2)}) %all-to-all-start.12) | async-done | bytes 1196064 | tf_op jit(solution)/shard_map/all_to_all | solution.py:15
  297.3 4.3 all-to-all-start.13
  305.1 8.9 %all-to-all-done.13 = bf16[8,584,128]{2,1,0:T(8,128)(2,1)} async-done(((bf16[8,584,128]{2,1,0:T(8,128)(2,1)}), bf16[8,584,128]{2,1,0:T(8,128)(2,1)}, u32[]{:S(2)}, u32[]{:S(2)}) %all-to-all-start.13) | async-done | bytes 1196064 | tf_op jit(solution)/shard_map/all_to_all | solution.py:50
  313.9 4.3 all-to-all-start.11
  321.9 8.9 %all-to-all-done.11 = bf16[8,584,128]{2,1,0:T(8,128)(2,1)} async-done(((bf16[8,584,128]{2,1,0:T(8,128)(2,1)}), bf16[8,584,128]{2,1,0:T(8,128)(2,1)}, u32[]{:S(2)}, u32[]{:S(2)}) %all-to-all-start.11) | async-done | bytes 1196064 | tf_op jit(solution)/shard_map/all_to_all | solution.py:50
  337.0 4.0 all-to-all-done.14
  345.2 4.5 all-to-all-start.15
  349.7 12.3 %all-to-all-done.15 = bf16[8,584,128]{2,1,0:T(8,128)(2,1)} async-done(((bf16[8,584,128]{2,1,0:T(8,128)(2,1)}), bf16[8,584,128]{2,1,0:T(8,128)(2,1)}, u32[]{:S(2)}, u32[]{:S(2)}) %all-to-all-start.15) | async-done | bytes 1196064 | tf_op jit(solution)/shard_map/all_to_all | solution.py:15
  376.6 15.1 %all_to_all.145 = bf16[8,584,128]{2,1,0:T(8,128)(2,1)S(1)} all-to-all(bf16[8,584,128]{2,1,0:T(8,128)(2,1)S(1)} %bitcast.375), channel_id=1, replica_groups=mesh['tok'=16,'wid'=8] {'wid'}, dimensions={0} | all-to-all | bytes 2392064 | tf_op jit(solution)/shard_map/all_to_all | solution.py:50
  393.4 8.8 %all_to_all.146 = f32[8,1,1168]{2,1,0:T(1,128)S(1)} all-to-all(f32[8,1,1168]{2,1,0:T(1,128)S(1)} %broadcast_in_dim.129), channel_id=1, replica_groups=mesh['tok'=16,'wid'=8] {'wid'}, dimensions={0} | all-to-all | bytes 74752 | tf_op jit(solution)/shard_map/all_to_all | solution.py:15
  406.3 4.2 all-to-all-start.18
  410.5 12.3 %all-to-all-done.18 = bf16[8,584,128]{2,1,0:T(8,128)(2,1)} async-done(((bf16[8,584,128]{2,1,0:T(8,128)(2,1)}), bf16[8,584,128]{2,1,0:T(8,128)(2,1)}, u32[]{:S(2)}, u32[]{:S(2)}) %all-to-all-start.18) | async-done | bytes 1196064 | tf_op jit(solution)/shard_map/all_to_all | solution.py:15
  429.5 4.7 all-to-all-start.19
  459.4 5.7 all-to-all-start.20
  482.9 5.8 all-to-all-start.21
  492.1 4.0 reshape.600
  510.8 3.7 reshape.594
  532.6 4.1 reshape.595
  538.2 3.7 all-to-all-start.25
  545.2 4.5 all-to-all-done.25
  549.7 5.6 all-to-all-start.22
  555.6 17.0 %reduce-scatter.5.cloned.1.call-done = bf16[768,128]{1,0:T(8,128)(2,1)} async-done(((bf16[12288,128]{1,0:T(8,128)(2,1)}), bf16[768,128]{1,0:T(8,128)(2,1)}) %reduce-scatter.5.cloned.1.call-update) | async-done | bytes 196624 | tf_op jit(solution)/shard_map/reduce_scatter | solution.py:71
  577.3 4.3 all-to-all-start.23
  581.7 6.2 all-to-all-done.23
  588.6 5.3 all-to-all-start.24
  595.1 6.6 all-to-all-done.24
  605.3 45.4 %reduce-scatter.3.cloned.1.call-done = bf16[768,128]{1,0:T(8,128)(2,1)} async-done(((bf16[12288,128]{1,0:T(8,128)(2,1)}), bf16[768,128]{1,0:T(8,128)(2,1)}) %reduce-scatter.3.cloned.1.call-update) | async-done | bytes 196624 | tf_op jit(solution)/shard_map/reduce_scatter | solution.py:71
  (388 shorter events, 217.9 us)
Async XLA Ops:
  7.2 10.6 %copy-start.53 = (f32[2,2,128]{2,1,0:T(2,128)S(1)}, f32[2,2,128]{2,1,0:T(2,128)}, u32[]{:S(2)}) copy-start(f32[2,2,128]{2,1,0:T(2,128)} %param.16) | copy-start | bytes 6148
  7.2 10.6 %copy-start.54 = (f32[2,2,128]{2,1,0:T(2,128)S(1)}, f32[2,2,128]{2,1,0:T(2,128)}, u32[]{:S(2)}) copy-start(f32[2,2,128]{2,1,0:T(2,128)} %param.15) | copy-start | bytes 6148
  7.2 57.7 %all-gather.3.cloned.1.call-start = ((), (), s32[]{:S(2)}) async-start(), calls=%async_computation.28 | async-start | bytes 3342336 | tf_op jit(solution)/shard_map/all_gather | solution.py:57
  12.4 11.8 %all-to-all-start = ((f32[8,1,1168]{2,1,0:T(1,128)}), f32[8,1,1168]{2,1,0:T(1,128)S(1)}, u32[]{:S(2)}, u32[]{:S(2)}) async-start(f32[8,1,1168]{2,1,0:T(1,128)} %broadcast_in_dim.60), calls=%async_computation | async-start | bytes 81920 | tf_op jit(solution)/shard_map/all_to_all | solution.py:15
  18.4 6.1 copy-start.37
  18.4 90.5 %copy-start.39 = (f32[128]{0:T(128)}, f32[128]{0:T(128)S(1)}, u32[]{:S(2)}) copy-start(f32[128]{0:T(128)S(1)} %get-tuple-element.188) | copy-start | bytes 1540
  18.4 163.0 %copy-start.41 = (f32[128]{0:T(128)}, f32[128]{0:T(128)S(1)}, u32[]{:S(2)}) copy-start(f32[128]{0:T(128)S(1)} %get-tuple-element.186) | copy-start | bytes 1540
  25.7 4.4 copy-start.35
  25.7 19.8 %all-to-all-start.1 = ((bf16[8,584,128]{2,1,0:T(8,128)(2,1)}), bf16[8,584,128]{2,1,0:T(8,128)(2,1)S(1)}, u32[]{:S(2)}, u32[]{:S(2)}) async-start(bf16[8,584,128]{2,1,0:T(8,128)(2,1)} %broadcast_in_dim.61), calls=%async_computation.1 | async-start | bytes 2392064 | tf_op jit(solution)/shard_map/all_to_all | solution.py:15
  30.0 39.3 %copy-start.44 = (f32[2,64]{1,0:T(2,128)}, f32[2,64]{1,0:T(2,128)S(1)}, u32[]{:S(2)}) copy-start(f32[2,64]{1,0:T(2,128)S(1)} %add.219) | copy-start | bytes 1540
  30.1 41.6 %copy-start.56 = (f32[2,64]{1,0:T(2,128)}, f32[2,64]{1,0:T(2,128)S(1)}, u32[]{:S(2)}) copy-start(f32[2,64]{1,0:T(2,128)S(1)} %add.216) | copy-start | bytes 1540
  47.1 19.3 %copy-start.19 = (bf16[584,1024,1]{1,0,2:T(8,128)(2,1)S(1)}, bf16[584,1024,1]{1,0,2:T(8,128)(2,1)}, u32[]{:S(2)}) copy-start(bf16[584,1024,1]{1,0,2:T(8,128)(2,1)} %reshape.601) | copy-start | bytes 3588100
  75.7 5.3 copy-start.62
  75.7 22.4 %all-to-all-start.2 = ((bf16[8,584,128]{2,1,0:T(8,128)(2,1)}), bf16[8,584,128]{2,1,0:T(8,128)(2,1)}, u32[]{:S(2)}, u32[]{:S(2)}) async-start(bf16[8,584,128]{2,1,0:T(8,128)(2,1)} %bitcast.368), calls=%async_computation.2 | async-start | bytes 2392064 | tf_op jit(solution)/shard_map/all_to_all | solution.py:50
  80.2 108.2 %all-gather.5.cloned.1.call-start = ((), (), s32[]{:S(2)}) async-start(), calls=%async_computation.29 | async-start | bytes 3342336 | tf_op jit(solution)/shard_map/all_gather | solution.py:57
  110.4 29.1 %all-to-all-start.4 = ((bf16[8,584,128]{2,1,0:T(8,128)(2,1)}), bf16[8,584,128]{2,1,0:T(8,128)(2,1)}, u32[]{:S(2)}, u32[]{:S(2)}) async-start(bf16[8,584,128]{2,1,0:T(8,128)(2,1)} %broadcast_in_dim.121), calls=%async_computation.4 | async-start | bytes 2392064 | tf_op jit(solution)/shard_map/all_to_all | solution.py:15
  148.8 4.9 copy-start.63
  148.8 21.2 %all-to-all-start.5 = ((bf16[8,584,128]{2,1,0:T(8,128)(2,1)}), bf16[8,584,128]{2,1,0:T(8,128)(2,1)}, u32[]{:S(2)}, u32[]{:S(2)}) async-start(bf16[8,584,128]{2,1,0:T(8,128)(2,1)} %bitcast.373), calls=%async_computation.5 | async-start | bytes 2392064 | tf_op jit(solution)/shard_map/all_to_all | solution.py:50
  183.8 4.5 copy-start.68
  183.8 20.0 %all-to-all-start.7 = ((bf16[8,584,128]{2,1,0:T(8,128)(2,1)}), bf16[8,584,128]{2,1,0:T(8,128)(2,1)}, u32[]{:S(2)}, u32[]{:S(2)}) async-start(bf16[8,584,128]{2,1,0:T(8,128)(2,1)} %broadcast_in_dim.123), calls=%async_computation.7 | async-start | bytes 2392064 | tf_op jit(solution)/shard_map/all_to_all | solution.py:15
  188.3 32.8 %copy-start.58 = (f32[2,64]{1,0:T(2,128)}, f32[2,64]{1,0:T(2,128)S(1)}, u32[]{:S(2)}) copy-start(f32[2,64]{1,0:T(2,128)S(1)} %add.241) | copy-start | bytes 1540
  188.3 30.2 %copy-start.46 = (f32[2,64]{1,0:T(2,128)}, f32[2,64]{1,0:T(2,128)S(1)}, u32[]{:S(2)}) copy-start(f32[2,64]{1,0:T(2,128)S(1)} %add.244) | copy-start | bytes 1540
  255.2 16.3 %copy-start.31 = (bf16[584,128]{1,0:T(8,128)(2,1)S(1)}, bf16[584,128]{1,0:T(8,128)(2,1)}, u32[]{:S(2)}) copy-start(bf16[584,128]{1,0:T(8,128)(2,1)} %param.25) | copy-start | bytes 448516
  272.7 4.6 copy-start.55
  272.7 17.4 %all-to-all-start.12 = ((bf16[8,584,128]{2,1,0:T(8,128)(2,1)}), bf16[8,584,128]{2,1,0:T(8,128)(2,1)}, u32[]{:S(2)}, u32[]{:S(2)}) async-start(bf16[8,584,128]{2,1,0:T(8,128)(2,1)} %broadcast_in_dim.126), calls=%async_computation.12 | async-start | bytes 2392064 | tf_op jit(solution)/shard_map/all_to_all | solution.py:15
  297.3 16.6 %all-to-all-start.13 = ((bf16[8,584,128]{2,1,0:T(8,128)(2,1)}), bf16[8,584,128]{2,1,0:T(8,128)(2,1)}, u32[]{:S(2)}, u32[]{:S(2)}) async-start(bf16[8,584,128]{2,1,0:T(8,128)(2,1)} %bitcast.372), calls=%async_computation.13 | async-start | bytes 2392064 | tf_op jit(solution)/shard_map/all_to_all | solution.py:50
  313.9 16.9 %all-to-all-start.11 = ((bf16[8,584,128]{2,1,0:T(8,128)(2,1)}), bf16[8,584,128]{2,1,0:T(8,128)(2,1)}, u32[]{:S(2)}, u32[]{:S(2)}) async-start(bf16[8,584,128]{2,1,0:T(8,128)(2,1)} %bitcast.370), calls=%async_computation.11 | async-start | bytes 2392064 | tf_op jit(solution)/shard_map/all_to_all | solution.py:50
  331.5 9.6 %all-to-all-start.14 = ((f32[8,1,1168]{2,1,0:T(1,128)}), f32[8,1,1168]{2,1,0:T(1,128)S(1)}, u32[]{:S(2)}, u32[]{:S(2)}) async-start(f32[8,1,1168]{2,1,0:T(1,128)} %broadcast_in_dim.127), calls=%async_computation.14 | async-start | bytes 81920 | tf_op jit(solution)/shard_map/all_to_all | solution.py:15
  345.2 16.8 %all-to-all-start.15 = ((bf16[8,584,128]{2,1,0:T(8,128)(2,1)}), bf16[8,584,128]{2,1,0:T(8,128)(2,1)}, u32[]{:S(2)}, u32[]{:S(2)}) async-start(bf16[8,584,128]{2,1,0:T(8,128)(2,1)} %broadcast_in_dim.128), calls=%async_computation.15 | async-start | bytes 2392064 | tf_op jit(solution)/shard_map/all_to_all | solution.py:15
  369.5 4.8 copy-start.23
  406.3 16.6 %all-to-all-start.18 = ((bf16[8,584,128]{2,1,0:T(8,128)(2,1)}), bf16[8,584,128]{2,1,0:T(8,128)(2,1)}, u32[]{:S(2)}, u32[]{:S(2)}) async-start(bf16[8,584,128]{2,1,0:T(8,128)(2,1)} %broadcast_in_dim.130), calls=%async_computation.18 | async-start | bytes 2392064 | tf_op jit(solution)/shard_map/all_to_all | solution.py:15
  429.5 25.9 %all-to-all-start.19 = ((bf16[8,584,128]{2,1,0:T(8,128)(2,1)}), bf16[8,584,128]{2,1,0:T(8,128)(2,1)}, u32[]{:S(2)}, u32[]{:S(2)}) async-start(bf16[8,584,128]{2,1,0:T(8,128)(2,1)} %bitcast.369), calls=%async_computation.19 | async-start | bytes 2392064 | tf_op jit(solution)/shard_map/all_to_all | solution.py:50
  459.4 19.4 %all-to-all-start.20 = ((f32[8,1,1168]{2,1,0:T(1,128)}), f32[8,1,1168]{2,1,0:T(1,128)S(1)}, u32[]{:S(2)}, u32[]{:S(2)}) async-start(f32[8,1,1168]{2,1,0:T(1,128)} %broadcast_in_dim.131), calls=%async_computation.20 | async-start | bytes 81920 | tf_op jit(solution)/shard_map/all_to_all | solution.py:15
  482.9 5.9 copy-start.22
  482.9 31.6 %all-to-all-start.21 = ((bf16[8,584,128]{2,1,0:T(8,128)(2,1)}), bf16[8,584,128]{2,1,0:T(8,128)(2,1)}, u32[]{:S(2)}, u32[]{:S(2)}) async-start(bf16[8,584,128]{2,1,0:T(8,128)(2,1)} %broadcast_in_dim.132), calls=%async_computation.21 | async-start | bytes 2392064 | tf_op jit(solution)/shard_map/all_to_all | solution.py:15
  488.7 83.9 %reduce-scatter.5.cloned.1.call-start = ((), (), s32[]{:S(2)}) async-start(), calls=%async_computation.31 | async-start | bytes 3342336 | tf_op jit(solution)/shard_map/reduce_scatter | solution.py:71
  496.1 154.6 %reduce-scatter.3.cloned.1.call-start = ((), (), s32[]{:S(2)}) async-start(), calls=%async_computation.30 | async-start | bytes 3342336 | tf_op jit(solution)/shard_map/reduce_scatter | solution.py:71
  536.7 5.2 copy-start.26
  536.7 5.2 copy-start.28
  536.7 5.2 copy-start.30
  538.2 11.5 %all-to-all-start.25 = ((f32[16,1,1536]{2,1,0:T(1,128)}), f32[16,1,1536]{2,1,0:T(1,128)S(1)}, u32[]{:S(2)}, u32[]{:S(2)}) async-start(f32[16,1,1536]{2,1,0:T(1,128)} %broadcast_in_dim.135), calls=%async_computation.25 | async-start | bytes 196608 | tf_op jit(solution)/shard_map/all_to_all | solution.py:15
  549.7 25.6 %all-to-all-start.22 = ((bf16[8,584,128]{2,1,0:T(8,128)(2,1)}), bf16[8,584,128]{2,1,0:T(8,128)(2,1)S(1)}, u32[]{:S(2)}, u32[]{:S(2)}) async-start(bf16[8,584,128]{2,1,0:T(8,128)(2,1)} %bitcast.351), calls=%async_computation.22 | async-start | bytes 2392064 | tf_op jit(solution)/shard_map/all_to_all | solution.py:50
  555.4 20.7 %copy-start.38 = (f32[128]{0:T(128)S(1)}, f32[128]{0:T(128)}, u32[]{:S(2)}) copy-start(f32[128]{0:T(128)} %copy-done.37) | copy-start | bytes 1540
  575.1 6.5 copy-start.67
  575.1 6.5 copy-start.66
  575.3 18.7 %copy-start.21 = (f32[584,128]{1,0:T(8,128)S(1)}, f32[584,128]{1,0:T(8,128)}, u32[]{:S(2)}) copy-start(f32[584,128]{1,0:T(8,128)} %get-tuple-element.97) | copy-start | bytes 897028
  577.3 10.6 %all-to-all-start.23 = ((f32[8,1,1168]{2,1,0:T(1,128)}), f32[8,1,1168]{2,1,0:T(1,128)S(1)}, u32[]{:S(2)}, u32[]{:S(2)}) async-start(f32[8,1,1168]{2,1,0:T(1,128)} %broadcast_in_dim.133), calls=%async_computation.23 | async-start | bytes 81920 | tf_op jit(solution)/shard_map/all_to_all | solution.py:15
  588.6 13.1 %all-to-all-start.24 = ((f32[16,1,1536]{2,1,0:T(1,128)}), f32[16,1,1536]{2,1,0:T(1,128)S(1)}, u32[]{:S(2)}, u32[]{:S(2)}) async-start(f32[16,1,1536]{2,1,0:T(1,128)} %broadcast_in_dim.134), calls=%async_computation.24 | async-start | bytes 196608 | tf_op jit(solution)/shard_map/all_to_all | solution.py:15
  (48 other events, 89.4 us)
Sparse Core Ops, SparseCore 0:
  11.5 53.3 all-gather.2
  84.1 59.2 all-gather.4
  496.2 76.2 reduce-scatter.4
  576.5 74.1 reduce-scatter.2
where the time goes:
time: 676 us; the launch traced here: 663 us
  waiting for transfers between devices  238 us (35%)
  local copies, waits for them, and re-layouts  111 us (16%)
  starting transfers between devices  87.8 us (13%)
  blocking collectives  84.3 us (12%)
  matrix products  81.4 us (12%)
  other arithmetic  45.3 us (7%)
  between operations  15.3 us (2%)
    all_to_all x13, waiting for transfers between devices, copy_for_each(): return lax.all_to_all(copies, axis, split_axis=0, concat_axis=0, tiled=True)  108 us
    reduce_scatter x2, waiting for transfers between devices, sum_together(): lax.psum_scatter(lines, axis, tiled=True).reshape(-1)  62.4 us
    all_to_all x13, starting transfers between devices, copy_for_each(): return lax.all_to_all(copies, axis, split_axis=0, concat_axis=0, tiled=True)  59.4 us
    all_to_all x5, blocking collectives, copy_for_each(): return lax.all_to_all(copies, axis, split_axis=0, concat_axis=0, tiled=True)  51.4 us
    all_to_all x6, waiting for transfers between devices, summed_on_arrival(): lax.all_to_all(tiles, axis, split_axis=0, concat_axis=0, tiled=True)  50.2 us
    all_to_all x2, blocking collectives, summed_on_arrival(): lax.all_to_all(tiles, axis, split_axis=0, concat_axis=0, tiled=True)  32.9 us
    all_to_all x6, starting transfers between devices, summed_on_arrival(): lax.all_to_all(tiles, axis, split_axis=0, concat_axis=0, tiled=True)  28.1 us
    dot_general x8, matrix products, contract_rows(): lax.dot_general(left, right, (((0,), (0,)), ((), ())), preferred_element_...  23.1 us
  transfers between devices with their start and end apart: 23, of which 18 were waited for; matrix products, arithmetic and copies ran while one was open for 21% of the time, Pallas kernels for 0%

commit v1 on v0

v1 whole, which is shorter than its diff:
```python
import functools

import jax
import jax.numpy as jnp
from jax import lax
from jax.experimental import pallas as pl
from jax.experimental.pallas import tpu as pltpu
from jax.sharding import PartitionSpec as P

HEAD = 64
LAYERS = 2
EPSILON = 1e-06
LANES = 128
BF16 = jnp.bfloat16
F32 = jnp.float32
VMEM_LIMIT = 20 * 1024 * 1024


def swap(value, axis, mask):
    pairs = [(i, i ^ mask) for i in range(lax.axis_size(axis))]
    return lax.ppermute(value, axis, pairs)


def gather_blocks(block):
    b1 = swap(block, "wid", 1)
    b2 = swap(block, "wid", 2)
    b6 = swap(block, "wid", 6)
    b4 = swap(block, "wid", 4)
    b3 = swap(b1, "wid", 2)
    b7 = swap(b1, "wid", 6)
    b5 = swap(b4, "wid", 1)
    return (block, b1, b2, b3, b4, b5, b6, b7)


def copies_to_all(value, axis):
    copies = jnp.broadcast_to(value, (lax.axis_size(axis), *value.shape))
    return lax.all_to_all(copies, axis, split_axis=0, concat_axis=0, tiled=True)


def add_up(*terms):
    return functools.reduce(jnp.add, [t.astype(F32) for t in terms])


def reduce_blocks(parts):
    for_pair = [swap(parts[3], "wid", 2), swap(parts[7], "wid", 6)]
    for_far = swap(parts[5], "wid", 1)
    near = [swap(parts[2], "wid", 2), swap(parts[6], "wid", 6)]
    far = swap(add_up(parts[4], for_far).astype(BF16), "wid", 4)
    pair = swap(add_up(parts[1], *for_pair).astype(BF16), "wid", 1)
    return add_up(parts[0], *near, far, pair)


def scatter_sum(parts):
    other = swap(parts[1], "tok", 1)
    sums = [add_up(parts[0, z], other[z]).astype(BF16) for z in range(4)]
    line = [swap(sums[z], "tok", 2 * z) for z in (2, 1, 3)]
    both = [add_up(sums[0][h], *[p[h] for p in line]) for h in range(2)]
    return both[0] + swap(both[1].astype(BF16), "tok", 8).astype(F32)


def dot_nn(a, b):
    return lax.dot_general(a, b, (((1,), (0,)), ((), ())), preferred_element_type=F32)


def dot_nt(a, b):
    return lax.dot_general(a, b, (((1,), (1,)), ((), ())), preferred_element_type=F32)


def dot_tn(a, b):
    return lax.dot_general(a, b, (((0,), (0,)), ((), ())), preferred_element_type=F32)


def over_rows(rows, size, body):
    count = rows // size

    def step(i, carry):
        body(pl.multiple_of(i * size, size), size)
        return carry

    lax.fori_loop(0, count, step, 0)
    if rows % size:
        body(count * size, rows % size)


def row_chunks(rows, count):
    step = rows // count // 16 * 16
    starts = [i * step for i in range(count)]
    return [(s, step if i + 1 < count else rows - s) for i, s in enumerate(starts)]


def place(me, slot):
    return pl.ds(pl.multiple_of((me ^ slot) * LANES, LANES), LANES)


def norm_rows(me, blocks, base, gains, shifts, x_ref, n_ref, xh_ref, r_ref):
    rows = n_ref.shape[0]
    count = len(blocks)
    width = count * LANES

    def body(start, size):
        at = pl.ds(start, size)
        vals = []
        for k, ref in enumerate(blocks):
            v = ref[at, :].astype(F32)
            if base is not None:
                v = v + base[at, place(me, k)]
            x_ref[at, place(me, k)] = v
            vals.append(v)
        mean = jnp.sum(functools.reduce(jnp.add, vals), axis=1, keepdims=True) / width
        vals = [v - mean for v in vals]
        spread = functools.reduce(jnp.add, [v * v for v in vals])
        spread = jnp.sum(spread, axis=1, keepdims=True) / width
        scale = lax.rsqrt(spread + EPSILON)
        r_ref[at, :] = jnp.broadcast_to(scale, (size, LANES))
        for k, v in enumerate(vals):
            xh = v * scale
            xh_ref[at, place(me, k)] = xh.astype(BF16)
            n_ref[at, place(me, k)] = (xh * gains(me ^ k) + shifts(me ^ k)).astype(BF16)

    over_rows(rows, 32, body)


def norm_back_rows(me, blocks, base, xh_ref, r_ref, g_ref, low_ref):
    rows = low_ref.shape[0]
    width = len(blocks) * LANES

    def body(start, size):
        at = pl.ds(start, size)
        vals = [ref[at, :].astype(F32) for ref in blocks]
        xhs = [xh_ref[at, place(me, k)].astype(F32) for k in range(len(blocks))]
        one = jnp.sum(functools.reduce(jnp.add, vals), axis=1, keepdims=True) / width
        two = functools.reduce(jnp.add, [v * x for v, x in zip(vals, xhs)])
        two = jnp.sum(two, axis=1, keepdims=True) / width
        scale = r_ref[at, :]
        for k, (v, x) in enumerate(zip(vals, xhs)):
            g = base[at, place(me, k)] + scale * (v - one - x * two)
            g_ref[at, place(me, k)] = g
            low_ref[at, place(me, k)] = g.astype(BF16)

    over_rows(rows, 32, body)


def partial_blocks(me, left, weight_ref, cols, part_refs):
    odd = lax.rem(me, 2) == 1
    for k in range(0, len(part_refs), 2):
        start = pl.multiple_of(((me // 2) ^ (k // 2)) * 2 * LANES, 2 * LANES)
        both = dot_nt(left, weight_ref[pl.ds(start, 2 * LANES), cols]).astype(BF16)
        low, high = both[:, :LANES], both[:, LANES:]
        part_refs[k][...] = jnp.where(odd, high, low)
        part_refs[k + 1][...] = jnp.where(odd, low, high)


def head_masks():
    lane = lax.broadcasted_iota(jnp.int32, (1, LANES), 1)
    return [(lane >= h * HEAD) & (lane < (h + 1) * HEAD) for h in range(LANES // HEAD)]


def head_scores(query, keys, allowed):
    return jnp.where(allowed, dot_nt(query, keys) * HEAD ** (-0.5), -1e30)


def erf_of(x):
    return lax.erf(x)


def attend_kernel(first, row, *refs):
    refs = list(refs)
    me_ref = refs[0]
    if first:
        par_ref = refs.pop()
        blocks, base, refs = refs[1:9], None, refs[9:]
        rows = blocks[0].shape[0] - 2 * par_ref.shape[1]
        for k, ref in enumerate(blocks):
            tail = ref[rows:, :].astype(F32)
            par_ref[me_ref[0] ^ k] = tail[: par_ref.shape[1]] + tail[par_ref.shape[1] :]
    else:
        par_ref, blocks, base, refs = refs[1], refs[2:10], refs[10], refs[11:]
    idr_ref, idc_ref, w_ref, qvb_ref = refs[:4]
    x_ref, n_ref, xh_ref, r_ref, qkv_ref, lse_ref, o_ref = refs[4:11]
    part_refs = refs[11:19]
    me = me_ref[0]
    rows = n_ref.shape[0]
    norm_rows(
        me,
        blocks,
        base,
        lambda j: par_ref[j, row : row + 1, :],
        lambda j: par_ref[j, row + 4 : row + 5, :],
        x_ref,
        n_ref,
        xh_ref,
        r_ref,
    )
    qkv = dot_nn(n_ref[...], w_ref[:, : 3 * LANES])
    qkv_ref[:, :LANES] = (qkv[:, :LANES] + qvb_ref[0:1, :]).astype(BF16)
    qkv_ref[:, LANES : 2 * LANES] = qkv[:, LANES : 2 * LANES].astype(BF16)
    qkv_ref[:, 2 * LANES :] = (qkv[:, 2 * LANES :] + qvb_ref[1:2, :]).astype(BF16)
    keys = qkv_ref[:, LANES : 2 * LANES]
    values = qkv_ref[:, 2 * LANES :]
    masks = head_masks()
    for start, size in row_chunks(rows, 4):
        query = qkv_ref[start : start + size, :LANES]
        allowed = idc_ref[start : start + size, :1] == idr_ref[...]
        mixed = jnp.zeros((size, LANES), F32)
        logsum = jnp.zeros((size, LANES), F32)
        for mask in masks:
            own = jnp.where(mask, query, jnp.zeros_like(query))
            scores = head_scores(own, keys, allowed)
            top = jnp.max(scores, axis=1, keepdims=True)
            expo = jnp.exp(scores - top)
            total = jnp.sum(expo, axis=1, keepdims=True)
            probs = (expo * (1.0 / total)).astype(BF16)
            mixed = jnp.where(mask, dot_nn(probs, values), mixed)
            logsum = jnp.where(mask, top + jnp.log(total), logsum)
        lse_ref[start : start + size, :] = logsum
        o_ref[start : start + size, :] = mixed.astype(BF16)
    partial_blocks(me, o_ref[...], w_ref, slice(3 * LANES, 4 * LANES), part_refs)


def feed_kernel(row, *refs):
    me_ref, par_ref = refs[:2]
    blocks = refs[2:10]
    base, w_ref, b_ref = refs[10:13]
    x_ref, n_ref, xh_ref, r_ref, h_ref, slope_ref = refs[13:19]
    part_refs, u_ref = refs[19:27], refs[27]
    me = me_ref[0]
    rows = n_ref.shape[0]
    ff = h_ref.shape[1]
    norm_rows(
        me,
        blocks,
        base,
        lambda j: par_ref[j, row : row + 1, :],
        lambda j: par_ref[j, row + 4 : row + 5, :],
        x_ref,
        n_ref,
        xh_ref,
        r_ref,
    )
    u_ref[...] = dot_nn(n_ref[...], w_ref[:, :ff])

    def body(start, size):
        at = pl.ds(start, size)
        u = u_ref[at, :] + b_ref[...]
        phi = 0.5 * (1.0 + erf_of(u * 0.7071067811865476))
        h_ref[at, :] = (u * phi).astype(BF16)
        slope_ref[at, :] = phi + u * jnp.exp(-0.5 * u * u) * 0.3989422804014327

    over_rows(rows, 32, body)
    partial_blocks(me, h_ref[...], w_ref, slice(ff, 2 * ff), part_refs)


def feed_back_kernel(first, *refs):
    refs = list(refs)
    me_ref = refs[0]
    blocks = refs[1:9]
    if first:
        w_ref, slope_ref, g_ref, low_ref, du_ref = refs[9:14]
    else:
        base, xh_ref, r_ref, w_ref, slope_ref, g_ref, low_ref, du_ref = refs[9:17]
    part_refs, dh_ref = refs[-9:-1], refs[-1]
    me = me_ref[0]
    rows, ff = slope_ref.shape
    if first:

        def copy(start, size):
            at = pl.ds(start, size)
            for k, ref in enumerate(blocks):
                low_ref[at, place(me, k)] = ref[at, :]
                g_ref[at, place(me, k)] = ref[at, :].astype(F32)

        over_rows(rows, 32, copy)
    else:
        norm_back_rows(me, blocks, base, xh_ref, r_ref, g_ref, low_ref)
    dh_ref[...] = dot_nn(low_ref[...], w_ref[:, ff:])

    def body(start, size):
        at = pl.ds(start, size)
        du_ref[at, :] = (dh_ref[at, :] * slope_ref[at, :]).astype(BF16)

    over_rows(rows, 32, body)
    partial_blocks(me, du_ref[...], w_ref, slice(0, ff), part_refs)


def attend_back_kernel(*refs):
    me_ref = refs[0]
    blocks = refs[1:9]
    base, xh_ref, r_ref, w_ref, qkv_ref, lse_ref, idr_ref, idc_ref = refs[9:17]
    g_ref, low_ref, dproj_ref = refs[17:20]
    part_refs = refs[20:28]
    do_ref, p_ref, ds_ref = refs[28:]
    me = me_ref[0]
    rows = low_ref.shape[0]
    norm_back_rows(me, blocks, base, xh_ref, r_ref, g_ref, low_ref)
    do_ref[...] = dot_nn(low_ref[...], w_ref[:, 3 * LANES :]).astype(BF16)
    keys = qkv_ref[:, LANES : 2 * LANES]
    values = qkv_ref[:, 2 * LANES :]
    scale = HEAD ** (-0.5)
    dk = jnp.zeros((rows, LANES), F32)
    dv = jnp.zeros((rows, LANES), F32)
    masks = head_masks()
    for h, mask in enumerate(masks):
        for start, size in row_chunks(rows, 4):
            end = start + size
            query = qkv_ref[start:end, :LANES]
            own = jnp.where(mask, query, jnp.zeros_like(query))
            allowed = idc_ref[start:end, :1] == idr_ref[...]
            scores = head_scores(own, keys, allowed)
            probs = jnp.exp(scores - lse_ref[start:end, h * HEAD : h * HEAD + 1])
            p_ref[start:end, :] = probs.astype(BF16)
            dmix = do_ref[start:end, :]
            dmix = jnp.where(mask, dmix, jnp.zeros_like(dmix))
            dprobs = dot_nt(dmix, values)
            centre = jnp.sum(probs * dprobs, axis=1, keepdims=True)
            ds = (probs * (dprobs - centre)).astype(BF16)
            ds_ref[start:end, :] = ds
            dq = (dot_nn(ds, keys) * scale).astype(BF16)
            if h == 0:
                dproj_ref[start:end, :LANES] = dq
            else:
                dproj_ref[start:end, :LANES] = jnp.where(mask, dq, dproj_ref[start:end, :LANES])
        dv = jnp.where(mask, dot_tn(p_ref[...], do_ref[...]), dv)
        dk = jnp.where(mask, dot_tn(ds_ref[...], qkv_ref[:, :LANES]), dk)
    dproj_ref[:, LANES : 2 * LANES] = (dk * scale).astype(BF16)
    dproj_ref[:, 2 * LANES :] = dv.astype(BF16)
    partial_blocks(me, dproj_ref[...], w_ref, slice(0, 3 * LANES), part_refs)


def weight_grad_kernel(me_ref, xa_ref, ya_ref, xb_ref, yb_ref, out_ref):
    split = ya_ref.shape[1]
    step = 256
    shard = xa_ref.shape[1] // 16
    me = me_ref[0]
    for i in range(0, xa_ref.shape[1], step):
        da = dot_tn(xa_ref[:, i : i + step], ya_ref[...]).astype(BF16)
        db = dot_tn(xb_ref[:, i : i + step], yb_ref[...]).astype(BF16)
        if len(out_ref.shape) == 2:
            out_ref[i : i + step, :split] = da
            out_ref[i : i + step, split:] = db
        else:
            for s in range(0, step, shard):
                to = me ^ ((i + s) // shard)
                c, z, h = to & 1, (to >> 1) & 3, to >> 3
                out_ref[c, z, h, :, :split] = da[s : s + shard]
                out_ref[c, z, h, :, split:] = db[s : s + shard]


def whole(kernel, outs, scratch, name, flops, *args):
    vmem = pl.BlockSpec(memory_space=pltpu.VMEM)
    smem = pl.BlockSpec(memory_space=pltpu.SMEM)
    size = sum(a.size * a.dtype.itemsize for a in args)
    size += sum(o.size * o.dtype.itemsize for o in outs)
    return pl.pallas_call(
        kernel,
        out_shape=outs,
        in_specs=[smem if a.shape == (1,) else vmem for a in args],
        out_specs=[vmem] * len(outs),
        scratch_shapes=scratch,
        compiler_params=pltpu.CompilerParams(vmem_limit_bytes=VMEM_LIMIT),
        cost_estimate=pl.CostEstimate(flops=flops, bytes_accessed=size, transcendentals=0),
        name=name,
    )(*args)


def shards(
    tokens,
    image_ids,
    norm_gains,
    norm_shifts,
    qkv_weight,
    qv_bias,
    out_weight,
    out_bias,
    up_weight,
    up_bias,
    down_weight,
    down_bias,
    out_grad,
):
    rows, cols = tokens.shape
    peers = lax.axis_size("wid")
    width = cols * peers
    ff = up_weight.shape[2]
    me = lax.axis_index("wid")
    me1 = me.astype(jnp.int32).reshape(1)

    def arr(shape, dtype):
        return jax.ShapeDtypeStruct(shape, dtype)

    full32 = arr((rows, width), F32)
    full16 = arr((rows, width), BF16)
    own32 = arr((rows, cols), F32)
    own16 = arr((rows, cols), BF16)
    parts16 = [own16] * peers
    met = lax.axis_index("tok").astype(jnp.int32).reshape(1)
    shard = width // lax.axis_size("tok")

    down_t = jnp.swapaxes(down_weight, 1, 2)
    out_t = jnp.swapaxes(out_weight, 1, 2)
    mix_local = [
        jnp.concatenate([qkv_weight[l].reshape(-1, 3 * cols), out_t[l]], axis=1)
        for l in range(LAYERS)
    ]
    feed_local = [jnp.concatenate([up_weight[l], down_t[l]], axis=1) for l in range(LAYERS)]

    small = jnp.concatenate([norm_gains.reshape(-1, cols), norm_shifts.reshape(-1, cols)])
    high = lax.reduce_precision(small, 8, 7)
    rest = lax.reduce_precision(small - high, 8, 7)
    blocks = gather_blocks(
        jnp.concatenate([tokens, high.astype(BF16), rest.astype(BF16)], axis=0)
    )
    mix_w = [copies_to_all(mix_local[0], "tok").reshape(width, 4 * cols)]
    pars = None
    feed_w = [lax.all_gather(feed_local[0], "tok", axis=0, tiled=True)]
    mix_w.append(lax.all_gather(mix_local[1], "tok", axis=0, tiled=True))
    feed_w.append(lax.all_gather(feed_local[1], "tok", axis=0, tiled=True))

    idr = image_ids.reshape(1, rows)
    idc = jnp.broadcast_to(image_ids[:, None], (rows, LANES))

    mm = 2 * rows * width
    base = None
    saved = []
    for l in range(LAYERS):
        first = base is None
        x, n1, xh1, r1, qkv, lse, o, *part = whole(
            functools.partial(attend_kernel, first, 2 * l),
            [full32, full16, full16, own32, arr((rows, 3 * cols), BF16), own32, own16, *parts16]
            + [arr((peers, *small.shape), F32)] * first,
            [],
            "attend",
            mm * 4 * cols + 8 * rows * rows * cols,
            me1,
            *(() if first else (pars,)),
            *blocks,
            *(() if first else (base,)),
            idr,
            idc,
            mix_w[l],
            qv_bias[l],
        )
        if first:
            pars = part.pop()
        blocks = gather_blocks((reduce_blocks(part) + out_bias[l]).astype(BF16))
        mid, n2, xh2, r2, h, slope, *part = whole(
            functools.partial(feed_kernel, 2 * l + 1),
            [
                full32,
                full16,
                full16,
                own32,
                arr((rows, ff), BF16),
                arr((rows, ff), F32),
                *parts16,
            ],
            [pltpu.VMEM((rows, ff), F32)],
            "feed",
            mm * 2 * ff,
            me1,
            pars,
            *blocks,
            x,
            feed_w[l],
            up_bias[l].reshape(1, ff),
        )
        branch = reduce_blocks(part) + down_bias[l]
        base = mid
        if l + 1 < LAYERS:
            blocks = gather_blocks(branch.astype(BF16))
        saved.append((n1, xh1, r1, qkv, lse, o, n2, xh2, r2, h, slope))
    state = lax.dynamic_slice_in_dim(base, me * cols, cols, 1) + branch
    activations = state.astype(BF16)

    blocks = gather_blocks(out_grad)
    g = None
    results = []
    for l in reversed(range(LAYERS)):
        n1, xh1, r1, qkv, lse, o, n2, xh2, r2, h, slope = saved[l]
        extra = () if g is None else (g, xh_up, r_up)
        g, gm, du, *part = whole(
            functools.partial(feed_back_kernel, g is None),
            [full32, full16, arr((rows, ff), BF16), *parts16],
            [pltpu.VMEM((rows, ff), F32)],
            "feed_back",
            mm * 2 * ff,
            me1,
            *blocks,
            *extra,
            feed_w[l],
            slope,
        )
        dn2 = reduce_blocks(part)
        blocks = gather_blocks((dn2 * norm_gains[l, 1]).astype(BF16))
        (dfeed,) = whole(
            weight_grad_kernel,
            [arr((width, 2 * ff) if l else (2, 4, 2, shard, 2 * ff), BF16)],
            [],
            "feed_grad",
            mm * 2 * ff,
            met,
            n2,
            du,
            gm,
            h,
        )
        g, ga, dproj, *part = whole(
            attend_back_kernel,
            [full32, full16, arr((rows, 3 * cols), BF16), *parts16],
            [
                pltpu.VMEM((rows, cols), BF16),
                pltpu.VMEM((rows, rows), BF16),
                pltpu.VMEM((rows, rows), BF16),
            ],
            "attend_back",
            mm * 4 * cols + 20 * rows * rows * cols,
            me1,
            *blocks,
            g,
            xh2,
            r2,
            mix_w[l],
            qkv,
            lse,
            idr,
            idc,
        )
        dn1 = reduce_blocks(part)
        (dmix,) = whole(
            weight_grad_kernel,
            [arr((width, 4 * cols) if l else (2, 4, 2, shard, 4 * cols), BF16)],
            [],
            "attend_grad",
            mm * 4 * cols,
            met,
            n1,
            dproj,
            ga,
            o,
        )
        own = lambda a: lax.dynamic_slice_in_dim(a, me * cols, cols, 1).astype(F32)
        xo1 = own(xh1)
        a1 = dn1 * norm_gains[l, 0]
        if l:
            blocks = gather_blocks(a1.astype(BF16))
            xh_up, r_up = xh1, r1
        else:
            sums = jnp.concatenate([jnp.sum(a1, axis=1), jnp.sum(a1 * xo1, axis=1)])
            sums = copies_to_all(sums.reshape(1, -1), "wid").sum(axis=0).reshape(-1)
            one, two = sums[:rows, None] / width, sums[rows:, None] / width
            input_grad = own(g) + r1 * (a1 - one - xo1 * two)
        vectors = [
            jnp.sum(dn1 * xo1, axis=0),
            jnp.sum(dn2 * own(xh2), axis=0),
            jnp.sum(dn1, axis=0),
            jnp.sum(dn2, axis=0),
            jnp.sum(dproj[:, :cols].astype(F32), axis=0),
            jnp.sum(dproj[:, 2 * cols :].astype(F32), axis=0),
            jnp.sum(own(ga), axis=0),
            jnp.sum(own(gm), axis=0),
            jnp.sum(du.astype(F32), axis=0),
        ]
        if l:
            scattered = [
                lax.psum_scatter(a, "tok", scatter_dimension=0, tiled=True).astype(F32)
                for a in (dfeed, dmix)
            ]
        else:
            scattered = [scatter_sum(dfeed), scatter_sum(dmix)]
        results.append((jnp.concatenate(vectors).reshape(-1, cols), scattered))
    results = results[::-1]
    lines = jnp.stack([line for line, _ in results])
    lines = copies_to_all(lines, "tok").reshape(-1, *lines.shape).sum(axis=0)
    results = [(lines[l], results[l][1]) for l in range(LAYERS)]

    def stack(pick):
        return jnp.stack([pick(line, big) for line, big in results])

    return (
        activations,
        input_grad,
        stack(lambda v, b: v[0:2]),
        stack(lambda v, b: v[2:4]),
        stack(lambda v, b: b[1][:, : 3 * cols].reshape(-1, 3, cols)),
        stack(lambda v, b: v[4:6]),
        jnp.swapaxes(stack(lambda v, b: b[1][:, 3 * cols :]), 1, 2),
        stack(lambda v, b: v[6]),
        stack(lambda v, b: b[0][:, :ff]),
        stack(lambda v, b: v[8:].reshape(-1)),
        jnp.swapaxes(stack(lambda v, b: b[0][:, ff:]), 1, 2),
        stack(lambda v, b: v[7]),
    )


def solution(mesh):
    placed = (
        P("tok", "wid"),
        P("tok"),
        P(None, None, "wid"),
        P(None, None, "wid"),
        P(None, "tok", None, "wid"),
        P(None, None, "wid"),
        P(None, "wid", "tok"),
        P(None, "wid"),
        P(None, "tok", "wid"),
        P(None, "wid"),
        P(None, "wid", "tok"),
        P(None, "wid"),
        P("tok", "wid"),
    )
    return jax.shard_map(
        shards,
        mesh=mesh,
        in_specs=placed,
        out_specs=(
            P("tok", "wid"),
            P("tok", "wid"),
            P(None, None, "wid"),
            P(None, None, "wid"),
            P(None, "tok", None, "wid"),
            P(None, None, "wid"),
            P(None, "wid", "tok"),
            P(None, "wid"),
            P(None, "tok", "wid"),
            P(None, "wid"),
            P(None, "wid", "tok"),
            P(None, "wid"),
        ),
        check_vma=False,
    )
```

time: 676 us -> 481 us (0.71)
  waiting for transfers between devices: 238 us -> 115 us
  starting transfers between devices: 87.8 us -> 173 us
  blocking collectives: 84.3 us -> 0 us
  matrix products: 81.4 us -> 0 us
  Pallas kernels: 0 us -> 68.9 us
  local copies, waits for them, and re-layouts: 111 us -> 68 us
  other arithmetic: 45.3 us -> 31.5 us
    ppermute x0 -> x122, starting transfers between devices: none -> 155 us  [swap(): return lax.ppermute(value, axis, pairs)]
    all_to_all x19 -> x3, waiting for transfers between devices: 158 us -> 6.13 us  [copies_to_all(): return lax.all_to_all(copies, axis, split_axis=0, concat_axis=0, tiled=True)]
    ppermute x0 -> x122, waiting for transfers between devices: none -> 108 us  [swap(): return lax.ppermute(value, axis, pairs)]
    all_to_all x7 -> x0, blocking collectives: 84.3 us -> none  [the longest x5 51.4 us: copy_for_each(): return lax.all_to_all(copies, axis, split_axis=0, concat_axis=0, tiled=True)]
    dot_general x36 -> x0, matrix products: 81.4 us -> none  [the longest x8 23.1 us: contract_rows(): lax.dot_general(left, right, (((0,), (0,)), ((), ())), preferred_element_...]
    all_to_all x19 -> x3, starting transfers between devices: 87.5 us -> 18.2 us  [copies_to_all(): return lax.all_to_all(copies, axis, split_axis=0, concat_axis=0, tiled=True)]
    pallas_call x0 -> x12, Pallas kernels: none -> 68.9 us  [whole(): pl.pallas_call(kernel, out_shape=outs, in_specs=[smem if a.shape == (1,)...]
    reduce_scatter x2, waiting for transfers between devices: 62.4 us -> 0.02 us  [shards(): lax.psum_scatter(a, 'tok', scatter_dimension=0, tiled=True).astype(F32)]
  transfers between devices with their start and end apart: 23 -> 130, of which waited for: 18 -> 55; matrix products, arithmetic and copies ran while one was open for 21% -> 8% of each run, Pallas kernels for 0% -> 11%
where the time goes in v1:
time: 481 us; the launch traced here: 472 us
  starting transfers between devices  173 us (36%)
  waiting for transfers between devices  115 us (24%)
  Pallas kernels  68.9 us (14%)
  local copies, waits for them, and re-layouts  68 us (14%)
  other arithmetic  31.5 us (7%)
  between operations  15.5 us (3%)
    ppermute x122, starting transfers between devices, swap(): return lax.ppermute(value, axis, pairs)  155 us
    ppermute x122, waiting for transfers between devices, swap(): return lax.ppermute(value, axis, pairs)  108 us
    pallas_call x12, Pallas kernels, whole(): pl.pallas_call(kernel, out_shape=outs, in_specs=[smem if a.shape == (1,)...  68.9 us
    unnamed x228, local copies, waits for them, and re-layouts  60 us
    all_to_all x3, starting transfers between devices, copies_to_all(): return lax.all_to_all(copies, axis, split_axis=0, concat_axis=0, tiled=True)  18.2 us
  transfers between devices with their start and end apart: 130, of which 55 were waited for; matrix products, arithmetic and copies ran while one was open for 8% of the time, Pallas kernels for 11%

profile of v1, /device:TPU:0, one launch (start us, length us, event | category | flops | bytes accessed | tf_op | source)
XLA Modules:
  0.0 472.1 jit_solution(510350935356424045)
XLA Ops:
  11.7 8.1 %all-to-all-start = ((bf16[16,64,512]{2,1,0:T(8,128)(2,1)}), bf16[16,64,512]{2,1,0:T(8,128)(2,1)S(1)}, u32[]{:S(2)}, u32[]{:S(2)}) async-start(bf16[16,64,512]{2,1,0:T(8,128)(2,1)} %broadcast_in_dim.18), calls=%async_computation | async-start | bytes 2097152 | tf_op jit(solution)/shard_map/all_to_all | solution.py:37
  20.6 3.2 collective-permute-start.3
  24.9 13.0 %collective-permute-done.refs_2_ = bf16[600,128]{1,0:T(8,128)(2,1)S(1)} collective-permute-done((bf16[600,128]{1,0:T(8,128)(2,1)S(1)}, bf16[600,128]{1,0:T(8,128)(2,1)S(1)}, u32[]{:S(2)}, u32[]{:S(2)}) %collective-permute-start) | collective-permute-done | bytes 153632 | tf_op jit(solution)/shard_map/ppermute | solution.py:21
  43.7 3.2 collective-permute-done.4.refs_6_
  47.1 9.3 %attend.2 = (f32[584,1024]{1,0:T(8,128)S(1)}, bf16[584,1024]{1,0:T(8,128)(2,1)S(1)}, bf16[584,1024]{1,0:T(8,128)(2,1)S(1)}, f32[584,128]{1,0:T(8,128)S(1)}, bf16...) custom-call(s32[1]{0:T(128)} %bitcast.refs_0_, ...), custom_call_target="tpu_custom_call" | custom-call | flops 961609728 | bytes 9788708 | tf_op jit(solution)/shard_map/attend/pallas_call | solution.py:353
  74.7 2.3 collective-permute-start.10
  77.8 3.7 collective-permute-done.10
  81.7 3.2 collective-permute-start.17
  92.0 3.1 collective-permute-done.18.refs_7_
  98.3 6.6 %feed.2 = (f32[584,1024]{1,0:T(8,128)S(1)}, bf16[584,1024]{1,0:T(8,128)(2,1)S(1)}, bf16[584,1024]{1,0:T(8,128)(2,1)S(1)}, f32[584,128]{1,0:T(8,128)S(1)}, bf16[5...) custom-call(s32[1]{0:T(128)} %bitcast.refs_0_, ...), custom_call_target="tpu_custom_call" | custom-call | flops 1224736768 | bytes 13793284 | tf_op jit(solution)/shard_map/feed/pallas_call | solution.py:353
  120.4 4.8 %collective-permute-done.27 = bf16[584,128]{1,0:T(8,128)(2,1)S(1)} collective-permute-done((bf16[584,128]{1,0:T(8,128)(2,1)S(1)}, bf16[584,128]{1,0:T(8,128)(2,1)S(1)}, u32[]{:S(2)}, u32[]{:S(2)}) %collective-permute-start.27) | collective-permute-done | bytes 149536 | tf_op jit(solution)/shard_map/ppermute | solution.py:21
  125.1 3.1 collective-permute-done.24
  140.9 2.6 collective-permute-done.34.refs_9_
  146.4 8.8 %attend.3 = (f32[584,1024]{1,0:T(8,128)S(1)}, bf16[584,1024]{1,0:T(8,128)(2,1)S(1)}, bf16[584,1024]{1,0:T(8,128)(2,1)S(1)}, f32[584,128]{1,0:T(8,128)S(1)}, bf16...) custom-call(s32[1]{0:T(128)} %bitcast.refs_0_, ...), custom_call_target="tpu_custom_call" | custom-call | flops 961609728 | bytes 12148004 | tf_op jit(solution)/shard_map/attend/pallas_call | solution.py:353
  166.5 2.4 collective-permute-start.38
  170.5 4.4 collective-permute-done.38
  176.1 3.2 collective-permute-start.45
  197.8 6.6 %feed.3 = (f32[584,1024]{1,0:T(8,128)S(1)}, bf16[584,1024]{1,0:T(8,128)(2,1)S(1)}, bf16[584,1024]{1,0:T(8,128)(2,1)S(1)}, f32[584,128]{1,0:T(8,128)S(1)}, bf16[5...) custom-call(s32[1]{0:T(128)} %bitcast.refs_0_, ...), custom_call_target="tpu_custom_call" | custom-call | flops 1224736768 | bytes 13793284 | tf_op jit(solution)/shard_map/feed/pallas_call | solution.py:353
  207.0 5.5 %feed_back.2 = (f32[584,1024]{1,0:T(8,128)S(1)}, bf16[584,1024]{1,0:T(8,128)(2,1)S(1)}, bf16[584,512]{1,0:T(8,128)(2,1)S(1)}, bf16[584,128]{1,0:T(8,128)(2,1)S(1...) custom-call(s32[1]{0:T(128)} %bitcast.refs_0_, ...), custom_call_target="tpu_custom_call" | custom-call | flops 1224736768 | bytes 9871364 | tf_op jit(solution)/shard_map/feed_back/pallas_call | solution.py:353
  221.6 3.4 collective-permute-done.68
  228.5 2.8 collective-permute-done.69
  231.3 3.8 collective-permute-done.66
  241.5 2.3 collective-permute-done.73.refs_5_
  247.0 2.3 collective-permute-done.74.refs_6_
  249.3 2.6 collective-permute-done.76.refs_8_
  257.8 9.6 %attend_back.2 = (f32[584,1024]{1,0:T(8,128)S(1)}, bf16[584,1024]{1,0:T(8,128)(2,1)S(1)}, bf16[584,384]{1,0:T(8,128)(2,1)S(1)}, bf16[584,128]{1,0:T(8,128)(2,1)S...) custom-call(s32[1]{0:T(128)} %bitcast.refs_0_, ...), custom_call_target="tpu_custom_call" | custom-call | flops 1485471744 | bytes 12413220 | tf_op jit(solution)/shard_map/attend_back/pallas_call | solution.py:353
  274.1 2.3 attend_grad.3
  286.2 3.2 feed_grad.3
  294.9 5.9 %collective-permute-done.82 = bf16[584,128]{1,0:T(8,128)(2,1)S(1)} collective-permute-done((bf16[584,128]{1,0:T(8,128)(2,1)}, bf16[584,128]{1,0:T(8,128)(2,1)S(1)}, u32[]{:S(2)}, u32[]{:S(2)}) %collective-permute-start.82) | collective-permute-done | bytes 149536 | tf_op jit(solution)/shard_map/ppermute | solution.py:21
  304.0 3.6 collective-permute-done.79
  311.7 2.7 collective-permute-start.80
  317.7 3.3 collective-permute-done.80
  323.1 3.0 collective-permute-start.87
  329.5 2.7 collective-permute-done.87.refs_5_
  334.0 3.3 collective-permute-done.88.refs_6_
  338.7 4.5 feed_back.3
  352.1 2.6 collective-permute-start.94
  378.4 2.2 collective-permute-done.102.refs_6_
  380.7 9.5 %attend_back.3 = (f32[584,1024]{1,0:T(8,128)S(1)}, bf16[584,1024]{1,0:T(8,128)(2,1)S(1)}, bf16[584,384]{1,0:T(8,128)(2,1)S(1)}, bf16[584,128]{1,0:T(8,128)(2,1)S...) custom-call(s32[1]{0:T(128)} %bitcast.refs_0_, ...), custom_call_target="tpu_custom_call" | custom-call | flops 1485471744 | bytes 12413220 | tf_op jit(solution)/shard_map/attend_back/pallas_call | solution.py:353
  403.4 3.5 collective-permute-done.108
  409.4 3.6 all-to-all-start.1
  413.2 6.1 %all-to-all-done.1 = f32[8,1,1168]{2,1,0:T(1,128)S(1)} async-done(((f32[8,1,1168]{2,1,0:T(1,128)}), f32[8,1,1168]{2,1,0:T(1,128)S(1)}, u32[]{:S(2)}, u32[]{:S(2)}) %all-to-all-start.1) | async-done | bytes 37408 | tf_op jit(solution)/shard_map/all_to_all | solution.py:37
  420.1 6.5 %all-to-all-start.2 = ((f32[16,2,12,128]{3,1,2,0:T(2,128)}), f32[16,2,12,128]{3,1,2,0:T(2,128)}, u32[]{:S(2)}, u32[]{:S(2)}) async-start(f32[16,2,12,128]{3,1,2,0:T(2,128)} %broadcast_in_dim.20), calls=%async_computation.2 | async-start | bytes 393216 | tf_op jit(solution)/shard_map/all_to_all | solution.py:37
  431.2 2.3 fusion.3
  433.5 3.1 collective-permute-start.120
  441.6 2.9 collective-permute-start.113
  450.6 3.5 collective-permute-start.116
  456.0 3.3 collective-permute-start.121
  (554 shorter events, 249.4 us)
Async XLA Ops:
  7.2 87.9 %all-gather.4.cloned.1.call-start = ((), (), s32[]{:S(2)}) async-start(), calls=%async_computation.5 | async-start | bytes 2228224 | tf_op jit(solution)/shard_map/all_gather | solution.py:414
  8.9 129.7 %all-gather.6.cloned.1.call-start = ((), (), s32[]{:S(2)}) async-start(), calls=%async_computation.6 | async-start | bytes 1114112 | tf_op jit(solution)/shard_map/all_gather | solution.py:415
  11.7 35.2 %all-to-all-start = ((bf16[16,64,512]{2,1,0:T(8,128)(2,1)}), bf16[16,64,512]{2,1,0:T(8,128)(2,1)S(1)}, u32[]{:S(2)}, u32[]{:S(2)}) async-start(bf16[16,64,512]{2,1,0:T(8,128)(2,1)} %broadcast_in_dim.18), calls=%async_computation | async-start | bytes 2097152 | tf_op jit(solution)/shard_map/all_to_all | solution.py:37
  19.8 174.7 %all-gather.8.cloned.1.call-start = ((), (), s32[]{:S(2)}) async-start(), calls=%async_computation.7 | async-start | bytes 2228224 | tf_op jit(solution)/shard_map/all_gather | solution.py:416
  19.9 17.9 %collective-permute-start = (bf16[600,128]{1,0:T(8,128)(2,1)S(1)}, bf16[600,128]{1,0:T(8,128)(2,1)S(1)}, u32[]{:S(2)}, u32[]{:S(2)}) collective-permute-start(bf16[600,128]{1,0:T(8,128)(2,1)S(1)} %pad_maximum_fusion.2.refs_1_), channel_id=1, source_target_pairs={{0,1},{1,0},{2,3},{3,2},{4,5},{5,4},{6,7},{7,6},{8,9},{9,8},{10,11... | collective-permute-start | bytes 460808 | tf_op jit(solution)/shard_map/ppermute | solution.py:21
  20.6 21.0 %collective-permute-start.3 = (bf16[600,128]{1,0:T(8,128)(2,1)S(1)}, bf16[600,128]{1,0:T(8,128)(2,1)S(1)}, u32[]{:S(2)}, u32[]{:S(2)}) collective-permute-start(bf16[600,128]{1,0:T(8,128)(2,1)S(1)} %pad_maximum_fusion.2.refs_1_), channel_id=1, source_target_pairs={{0,4},{1,5},{2,6},{3,7},{4,0},{5,1},{6,2},{7,3},{8,12},{9,13},{10,... | collective-permute-start | bytes 460808 | tf_op jit(solution)/shard_map/ppermute | solution.py:21
  23.8 19.2 %collective-permute-start.1 = (bf16[600,128]{1,0:T(8,128)(2,1)S(1)}, bf16[600,128]{1,0:T(8,128)(2,1)S(1)}, u32[]{:S(2)}, u32[]{:S(2)}) collective-permute-start(bf16[600,128]{1,0:T(8,128)(2,1)S(1)} %pad_maximum_fusion.2.refs_1_), channel_id=1, source_target_pairs={{0,2},{1,3},{2,0},{3,1},{4,6},{5,7},{6,4},{7,5},{8,10},{9,11},{10,... | collective-permute-start | bytes 460808 | tf_op jit(solution)/shard_map/ppermute | solution.py:21
  24.5 18.6 %collective-permute-start.5 = (bf16[600,128]{1,0:T(8,128)(2,1)S(1)}, bf16[600,128]{1,0:T(8,128)(2,1)S(1)}, u32[]{:S(2)}, u32[]{:S(2)}) collective-permute-start(bf16[600,128]{1,0:T(8,128)(2,1)S(1)} %pad_maximum_fusion.2.refs_1_), channel_id=1, source_target_pairs={{0,6},{1,7},{2,4},{3,5},{4,2},{5,3},{6,0},{7,1},{8,14},{9,15},{10,... | collective-permute-start | bytes 460808 | tf_op jit(solution)/shard_map/ppermute | solution.py:21
  66.9 361.9 %reduce-scatter.3.cloned.1.call-start = ((), (), s32[]{:S(2)}) async-start(), calls=%async_computation.8 | async-start | bytes 1114112 | tf_op jit(solution)/shard_map/reduce_scatter | solution.py:564
  129.9 8.7 %collective-permute-start.29 = (bf16[584,128]{1,0:T(8,128)(2,1)S(1)}, bf16[584,128]{1,0:T(8,128)(2,1)S(1)}, u32[]{:S(2)}, u32[]{:S(2)}) collective-permute-start(bf16[584,128]{1,0:T(8,128)(2,1)S(1)} %add_convert_fusion.14.refs_2_), channel_id=1, source_target_pairs={{0,2},{1,3},{2,0},{3,1},{4,6},{5,7},{6,4},{7,5},{8,10},{9,11},{10,... | collective-permute-start | bytes 448520 | tf_op jit(solution)/shard_map/ppermute | solution.py:21
  161.0 9.5 %collective-permute-start.36 = (bf16[584,128]{1,0:T(8,128)(2,1)S(1)}, bf16[584,128]{1,0:T(8,128)(2,1)S(1)}, u32[]{:S(2)}, u32[]{:S(2)}) collective-permute-start(bf16[584,128]{1,0:T(8,128)(2,1)S(1)} %get-tuple-element.136), channel_id=1, source_target_pairs={{0,6},{1,7},{2,4},{3,5},{4,2},{5,3},{6,0},{7,1},{8,14},{9,15},{10,... | collective-permute-start | bytes 448520 | tf_op jit(solution)/shard_map/ppermute | solution.py:21
  168.9 13.3 %collective-permute-start.56 = (bf16[584,128]{1,0:T(8,128)(2,1)S(1)}, bf16[584,128]{1,0:T(8,128)(2,1)}, u32[]{:S(2)}, u32[]{:S(2)}) collective-permute-start(bf16[584,128]{1,0:T(8,128)(2,1)S(1)} %copy-done.77), channel_id=1, source_target_pairs={{0,1},{1,0},{2,3},{3,2},{4,5},{5,4},{6,7},{7,6},{8,9},{9,8},{10,11... | collective-permute-start | bytes 448520 | tf_op jit(solution)/shard_map/ppermute | solution.py:21
  188.1 18.8 %collective-permute-start.57 = (bf16[584,128]{1,0:T(8,128)(2,1)S(1)}, bf16[584,128]{1,0:T(8,128)(2,1)}, u32[]{:S(2)}, u32[]{:S(2)}) collective-permute-start(bf16[584,128]{1,0:T(8,128)(2,1)S(1)} %copy-done.77), channel_id=1, source_target_pairs={{0,2},{1,3},{2,0},{3,1},{4,6},{5,7},{6,4},{7,5},{8,10},{9,11},{10,... | collective-permute-start | bytes 448520 | tf_op jit(solution)/shard_map/ppermute | solution.py:21
  188.6 18.3 %collective-permute-start.61 = (bf16[584,128]{1,0:T(8,128)(2,1)S(1)}, bf16[584,128]{1,0:T(8,128)(2,1)}, u32[]{:S(2)}, u32[]{:S(2)}) collective-permute-start(bf16[584,128]{1,0:T(8,128)(2,1)S(1)} %copy-done.77), channel_id=1, source_target_pairs={{0,6},{1,7},{2,4},{3,5},{4,2},{5,3},{6,0},{7,1},{8,14},{9,15},{10,... | collective-permute-start | bytes 448520 | tf_op jit(solution)/shard_map/ppermute | solution.py:21
  189.8 17.1 %collective-permute-start.58 = (bf16[584,128]{1,0:T(8,128)(2,1)}, bf16[584,128]{1,0:T(8,128)(2,1)}, u32[]{:S(2)}, u32[]{:S(2)}) collective-permute-start(bf16[584,128]{1,0:T(8,128)(2,1)} %collective-permute-done.56.refs_2_), channel_id=1, source_target_pairs={{0,2},{1,3},{2,0},{3,1},{4,6},{5,7},{6,4},{7,5},{8,10},{9,11},{10,... | collective-permute-start | bytes 448520 | tf_op jit(solution)/shard_map/ppermute | solution.py:21
  190.9 16.0 %collective-permute-start.60 = (bf16[584,128]{1,0:T(8,128)(2,1)}, bf16[584,128]{1,0:T(8,128)(2,1)}, u32[]{:S(2)}, u32[]{:S(2)}) collective-permute-start(bf16[584,128]{1,0:T(8,128)(2,1)} %collective-permute-done.59.refs_5_), channel_id=1, source_target_pairs={{0,1},{1,0},{2,3},{3,2},{4,5},{5,4},{6,7},{7,6},{8,9},{9,8},{10,11... | collective-permute-start | bytes 448520 | tf_op jit(solution)/shard_map/ppermute | solution.py:21
  192.5 14.4 %collective-permute-start.62 = (bf16[584,128]{1,0:T(8,128)(2,1)}, bf16[584,128]{1,0:T(8,128)(2,1)}, u32[]{:S(2)}, u32[]{:S(2)}) collective-permute-start(bf16[584,128]{1,0:T(8,128)(2,1)} %collective-permute-done.56.refs_2_), channel_id=1, source_target_pairs={{0,6},{1,7},{2,4},{3,5},{4,2},{5,3},{6,0},{7,1},{8,14},{9,15},{10,... | collective-permute-start | bytes 448520 | tf_op jit(solution)/shard_map/ppermute | solution.py:21
  216.4 8.6 %collective-permute-start.68 = (bf16[584,128]{1,0:T(8,128)(2,1)}, bf16[584,128]{1,0:T(8,128)(2,1)S(1)}, u32[]{:S(2)}, u32[]{:S(2)}) collective-permute-start(bf16[584,128]{1,0:T(8,128)(2,1)} %get-tuple-element.160), channel_id=1, source_target_pairs={{0,6},{1,7},{2,4},{3,5},{4,2},{5,3},{6,0},{7,1},{8,14},{9,15},{10,... | collective-permute-start | bytes 448520 | tf_op jit(solution)/shard_map/ppermute | solution.py:21
  217.7 9.7 %collective-permute-start.65 = (bf16[584,128]{1,0:T(8,128)(2,1)}, bf16[584,128]{1,0:T(8,128)(2,1)S(1)}, u32[]{:S(2)}, u32[]{:S(2)}) collective-permute-start(bf16[584,128]{1,0:T(8,128)(2,1)} %get-tuple-element.157), channel_id=1, source_target_pairs={{0,1},{1,0},{2,3},{3,2},{4,5},{5,4},{6,7},{7,6},{8,9},{9,8},{10,11... | collective-permute-start | bytes 448520 | tf_op jit(solution)/shard_map/ppermute | solution.py:21
  218.2 10.2 %collective-permute-start.64 = (bf16[584,128]{1,0:T(8,128)(2,1)}, bf16[584,128]{1,0:T(8,128)(2,1)S(1)}, u32[]{:S(2)}, u32[]{:S(2)}) collective-permute-start(bf16[584,128]{1,0:T(8,128)(2,1)} %get-tuple-element.155), channel_id=1, source_target_pairs={{0,6},{1,7},{2,4},{3,5},{4,2},{5,3},{6,0},{7,1},{8,14},{9,15},{10,... | collective-permute-start | bytes 448520 | tf_op jit(solution)/shard_map/ppermute | solution.py:21
  237.9 8.8 %collective-permute-start.71 = (bf16[584,128]{1,0:T(8,128)(2,1)S(1)}, bf16[584,128]{1,0:T(8,128)(2,1)}, u32[]{:S(2)}, u32[]{:S(2)}) collective-permute-start(bf16[584,128]{1,0:T(8,128)(2,1)S(1)} %multiply_convert_fusion.2.refs_1_), channel_id=1, source_target_pairs={{0,2},{1,3},{2,0},{3,1},{4,6},{5,7},{6,4},{7,5},{8,10},{9,11},{10,... | collective-permute-start | bytes 448520 | tf_op jit(solution)/shard_map/ppermute | solution.py:21
  278.3 184.5 %reduce-scatter.5.cloned.1.call-start = ((), (), s32[]{:S(2)}) async-start(), calls=%async_computation.9 | async-start | bytes 2228224 | tf_op jit(solution)/shard_map/reduce_scatter | solution.py:564
  278.3 11.4 %collective-permute-start.54 = (bf16[584,128]{1,0:T(8,128)(2,1)}, bf16[584,128]{1,0:T(8,128)(2,1)}, u32[]{:S(2)}, u32[]{:S(2)}) collective-permute-start(bf16[584,128]{1,0:T(8,128)(2,1)} %copy-done.83), channel_id=1, source_target_pairs={{0,6},{1,7},{2,4},{3,5},{4,2},{5,3},{6,0},{7,1},{8,14},{9,15},{10,... | collective-permute-start | bytes 448520 | tf_op jit(solution)/shard_map/ppermute | solution.py:21
  279.9 9.8 %collective-permute-start.53 = (bf16[584,128]{1,0:T(8,128)(2,1)}, bf16[584,128]{1,0:T(8,128)(2,1)}, u32[]{:S(2)}, u32[]{:S(2)}) collective-permute-start(bf16[584,128]{1,0:T(8,128)(2,1)} %copy-done.82), channel_id=1, source_target_pairs={{0,2},{1,3},{2,0},{3,1},{4,6},{5,7},{6,4},{7,5},{8,10},{9,11},{10,... | collective-permute-start | bytes 448520 | tf_op jit(solution)/shard_map/ppermute | solution.py:21
  279.9 13.8 %collective-permute-start.51 = (bf16[584,128]{1,0:T(8,128)(2,1)}, bf16[584,128]{1,0:T(8,128)(2,1)}, u32[]{:S(2)}, u32[]{:S(2)}) collective-permute-start(bf16[584,128]{1,0:T(8,128)(2,1)} %copy-done.81), channel_id=1, source_target_pairs={{0,1},{1,0},{2,3},{3,2},{4,5},{5,4},{6,7},{7,6},{8,9},{9,8},{10,11... | collective-permute-start | bytes 448520 | tf_op jit(solution)/shard_map/ppermute | solution.py:21
  280.7 29.7 %collective-permute-start.50 = (bf16[584,128]{1,0:T(8,128)(2,1)}, bf16[584,128]{1,0:T(8,128)(2,1)}, u32[]{:S(2)}, u32[]{:S(2)}) collective-permute-start(bf16[584,128]{1,0:T(8,128)(2,1)} %copy-done.80), channel_id=1, source_target_pairs={{0,6},{1,7},{2,4},{3,5},{4,2},{5,3},{6,0},{7,1},{8,14},{9,15},{10,... | collective-permute-start | bytes 448520 | tf_op jit(solution)/shard_map/ppermute | solution.py:21
  282.4 28.3 %collective-permute-start.49 = (bf16[584,128]{1,0:T(8,128)(2,1)}, bf16[584,128]{1,0:T(8,128)(2,1)}, u32[]{:S(2)}, u32[]{:S(2)}) collective-permute-start(bf16[584,128]{1,0:T(8,128)(2,1)} %copy-done.79), channel_id=1, source_target_pairs={{0,2},{1,3},{2,0},{3,1},{4,6},{5,7},{6,4},{7,5},{8,10},{9,11},{10,... | collective-permute-start | bytes 448520 | tf_op jit(solution)/shard_map/ppermute | solution.py:21
  290.9 20.8 %collective-permute-start.55 = (bf16[584,128]{1,0:T(8,128)(2,1)S(1)}, bf16[584,128]{1,0:T(8,128)(2,1)S(1)}, u32[]{:S(2)}, u32[]{:S(2)}) collective-permute-start(bf16[584,128]{1,0:T(8,128)(2,1)S(1)} %add_convert_fusion.9), channel_id=1, source_target_pairs={{0,1},{1,0},{2,3},{3,2},{4,5},{5,4},{6,7},{7,6},{8,9},{9,8},{10,11... | collective-permute-start | bytes 448520 | tf_op jit(solution)/shard_map/ppermute | solution.py:21
  292.2 8.6 %collective-permute-start.82 = (bf16[584,128]{1,0:T(8,128)(2,1)}, bf16[584,128]{1,0:T(8,128)(2,1)S(1)}, u32[]{:S(2)}, u32[]{:S(2)}) collective-permute-start(bf16[584,128]{1,0:T(8,128)(2,1)} %copy-done.88), channel_id=1, source_target_pairs={{0,6},{1,7},{2,4},{3,5},{4,2},{5,3},{6,0},{7,1},{8,14},{9,15},{10,... | collective-permute-start | bytes 448520 | tf_op jit(solution)/shard_map/ppermute | solution.py:21
  300.8 13.6 %collective-permute-start.52 = (bf16[584,128]{1,0:T(8,128)(2,1)S(1)}, bf16[584,128]{1,0:T(8,128)(2,1)S(1)}, u32[]{:S(2)}, u32[]{:S(2)}) collective-permute-start(bf16[584,128]{1,0:T(8,128)(2,1)S(1)} %add_convert_fusion.10), channel_id=1, source_target_pairs={{0,4},{1,5},{2,6},{3,7},{4,0},{5,1},{6,2},{7,3},{8,12},{9,13},{10,... | collective-permute-start | bytes 448520 | tf_op jit(solution)/shard_map/ppermute | solution.py:21
  307.7 9.9 %collective-permute-start.78 = (bf16[584,128]{1,0:T(8,128)(2,1)}, bf16[584,128]{1,0:T(8,128)(2,1)S(1)}, u32[]{:S(2)}, u32[]{:S(2)}) collective-permute-start(bf16[584,128]{1,0:T(8,128)(2,1)} %copy-done.85), channel_id=1, source_target_pairs={{0,6},{1,7},{2,4},{3,5},{4,2},{5,3},{6,0},{7,1},{8,14},{9,15},{10,... | collective-permute-start | bytes 448520 | tf_op jit(solution)/shard_map/ppermute | solution.py:21
  311.7 9.2 %collective-permute-start.80 = (bf16[584,128]{1,0:T(8,128)(2,1)S(1)}, bf16[584,128]{1,0:T(8,128)(2,1)S(1)}, u32[]{:S(2)}, u32[]{:S(2)}) collective-permute-start(bf16[584,128]{1,0:T(8,128)(2,1)S(1)} %add_convert_fusion.5), channel_id=1, source_target_pairs={{0,4},{1,5},{2,6},{3,7},{4,0},{5,1},{6,2},{7,3},{8,12},{9,13},{10,... | collective-permute-start | bytes 448520 | tf_op jit(solution)/shard_map/ppermute | solution.py:21
  323.1 9.7 %collective-permute-start.85 = (bf16[584,128]{1,0:T(8,128)(2,1)S(1)}, bf16[584,128]{1,0:T(8,128)(2,1)S(1)}, u32[]{:S(2)}, u32[]{:S(2)}) collective-permute-start(bf16[584,128]{1,0:T(8,128)(2,1)S(1)} %multiply_convert_fusion.1.refs_1_), channel_id=1, source_target_pairs={{0,2},{1,3},{2,0},{3,1},{4,6},{5,7},{6,4},{7,5},{8,10},{9,11},{10,... | collective-permute-start | bytes 448520 | tf_op jit(solution)/shard_map/ppermute | solution.py:21
  323.1 9.1 %collective-permute-start.87 = (bf16[584,128]{1,0:T(8,128)(2,1)S(1)}, bf16[584,128]{1,0:T(8,128)(2,1)S(1)}, u32[]{:S(2)}, u32[]{:S(2)}) collective-permute-start(bf16[584,128]{1,0:T(8,128)(2,1)S(1)} %multiply_convert_fusion.1.refs_1_), channel_id=1, source_target_pairs={{0,4},{1,5},{2,6},{3,7},{4,0},{5,1},{6,2},{7,3},{8,12},{9,13},{10,... | collective-permute-start | bytes 448520 | tf_op jit(solution)/shard_map/ppermute | solution.py:21
  327.9 9.5 %collective-permute-start.90 = (bf16[584,128]{1,0:T(8,128)(2,1)S(1)}, bf16[584,128]{1,0:T(8,128)(2,1)S(1)}, u32[]{:S(2)}, u32[]{:S(2)}) collective-permute-start(bf16[584,128]{1,0:T(8,128)(2,1)S(1)} %collective-permute-done.84.refs_2_), channel_id=1, source_target_pairs={{0,6},{1,7},{2,4},{3,5},{4,2},{5,3},{6,0},{7,1},{8,14},{9,15},{10,... | collective-permute-start | bytes 448520 | tf_op jit(solution)/shard_map/ppermute | solution.py:21
  360.6 12.5 %collective-permute-start.98 = (bf16[584,128]{1,0:T(8,128)(2,1)}, bf16[584,128]{1,0:T(8,128)(2,1)}, u32[]{:S(2)}, u32[]{:S(2)}) collective-permute-start(bf16[584,128]{1,0:T(8,128)(2,1)} %multiply_convert_fusion.refs_1_), channel_id=1, source_target_pairs={{0,1},{1,0},{2,3},{3,2},{4,5},{5,4},{6,7},{7,6},{8,9},{9,8},{10,11... | collective-permute-start | bytes 448520 | tf_op jit(solution)/shard_map/ppermute | solution.py:21
  362.1 13.2 %collective-permute-start.101 = (bf16[584,128]{1,0:T(8,128)(2,1)}, bf16[584,128]{1,0:T(8,128)(2,1)}, u32[]{:S(2)}, u32[]{:S(2)}) collective-permute-start(bf16[584,128]{1,0:T(8,128)(2,1)} %multiply_convert_fusion.refs_1_), channel_id=1, source_target_pairs={{0,4},{1,5},{2,6},{3,7},{4,0},{5,1},{6,2},{7,3},{8,12},{9,13},{10,... | collective-permute-start | bytes 448520 | tf_op jit(solution)/shard_map/ppermute | solution.py:21
  377.8 53.3 %collective-permute-start.117 = (bf16[4,2,64,1024]{3,2,1,0:T(8,128)(2,1)}, bf16[4,2,64,1024]{3,2,1,0:T(8,128)(2,1)}, u32[]{:S(2)}, u32[]{:S(2)}) collective-permute-start(bf16[4,2,64,1024]{3,2,1,0:T(8,128)(2,1)} %slice_bitcast_fusion), channel_id=1, source_target_pairs={{0,8},{8,0},{16,24},{24,16},{32,40},{40,32},{48,56},{56,48},{64,72... | collective-permute-start | bytes 3145736 | tf_op jit(solution)/shard_map/ppermute | solution.py:21
  393.5 9.5 %collective-permute-start.106 = (bf16[584,128]{1,0:T(8,128)(2,1)S(1)}, bf16[584,128]{1,0:T(8,128)(2,1)S(1)}, u32[]{:S(2)}, u32[]{:S(2)}) collective-permute-start(bf16[584,128]{1,0:T(8,128)(2,1)S(1)} %get-tuple-element.195), channel_id=1, source_target_pairs={{0,6},{1,7},{2,4},{3,5},{4,2},{5,3},{6,0},{7,1},{8,14},{9,15},{10,... | collective-permute-start | bytes 448520 | tf_op jit(solution)/shard_map/ppermute | solution.py:21
  403.0 35.0 %collective-permute-start.112 = (bf16[4,2,64,512]{3,2,1,0:T(8,128)(2,1)}, bf16[4,2,64,512]{3,2,1,0:T(8,128)(2,1)}, u32[]{:S(2)}, u32[]{:S(2)}) collective-permute-start(bf16[4,2,64,512]{3,2,1,0:T(8,128)(2,1)} %slice_bitcast_fusion.1), channel_id=1, source_target_pairs={{0,8},{8,0},{16,24},{24,16},{32,40},{40,32},{48,56},{56,48},{64,72... | collective-permute-start | bytes 1572872 | tf_op jit(solution)/shard_map/ppermute | solution.py:21
  409.4 9.9 %all-to-all-start.1 = ((f32[8,1,1168]{2,1,0:T(1,128)}), f32[8,1,1168]{2,1,0:T(1,128)S(1)}, u32[]{:S(2)}, u32[]{:S(2)}) async-start(f32[8,1,1168]{2,1,0:T(1,128)} %broadcast_in_dim.19), calls=%async_computation.1 | async-start | bytes 81920 | tf_op jit(solution)/shard_map/all_to_all | solution.py:37
  420.1 16.8 %all-to-all-start.2 = ((f32[16,2,12,128]{3,1,2,0:T(2,128)}), f32[16,2,12,128]{3,1,2,0:T(2,128)}, u32[]{:S(2)}, u32[]{:S(2)}) async-start(f32[16,2,12,128]{3,1,2,0:T(2,128)} %broadcast_in_dim.20), calls=%async_computation.2 | async-start | bytes 393216 | tf_op jit(solution)/shard_map/all_to_all | solution.py:37
  433.5 20.6 %collective-permute-start.120 = (bf16[2,64,1024]{2,1,0:T(8,128)(2,1)}, bf16[2,64,1024]{2,1,0:T(8,128)(2,1)S(1)}, u32[]{:S(2)}, u32[]{:S(2)}) collective-permute-start(bf16[2,64,1024]{2,1,0:T(8,128)(2,1)} %get-tuple-element.299), channel_id=1, source_target_pairs={{0,48},{8,56},{16,32},{24,40},{32,16},{40,24},{48,0},{56,8},{64,11... | collective-permute-start | bytes 786440 | tf_op jit(solution)/shard_map/ppermute | solution.py:21
  436.6 17.5 %collective-permute-start.119 = (bf16[2,64,1024]{2,1,0:T(8,128)(2,1)}, bf16[2,64,1024]{2,1,0:T(8,128)(2,1)S(1)}, u32[]{:S(2)}, u32[]{:S(2)}) collective-permute-start(bf16[2,64,1024]{2,1,0:T(8,128)(2,1)} %get-tuple-element.300), channel_id=1, source_target_pairs={{0,16},{8,24},{16,0},{24,8},{32,48},{40,56},{48,32},{56,40},{64,80... | collective-permute-start | bytes 786440 | tf_op jit(solution)/shard_map/ppermute | solution.py:21
  441.0 9.6 %collective-permute-start.114 = (bf16[2,64,512]{2,1,0:T(8,128)(2,1)S(1)}, bf16[2,64,512]{2,1,0:T(8,128)(2,1)S(1)}, u32[]{:S(2)}, u32[]{:S(2)}) collective-permute-start(bf16[2,64,512]{2,1,0:T(8,128)(2,1)S(1)} %get-tuple-element.304), channel_id=1, source_target_pairs={{0,16},{8,24},{16,0},{24,8},{32,48},{40,56},{48,32},{56,40},{64,80... | collective-permute-start | bytes 393224 | tf_op jit(solution)/shard_map/ppermute | solution.py:21
  441.6 9.0 %collective-permute-start.113 = (bf16[2,64,512]{2,1,0:T(8,128)(2,1)S(1)}, bf16[2,64,512]{2,1,0:T(8,128)(2,1)S(1)}, u32[]{:S(2)}, u32[]{:S(2)}) collective-permute-start(bf16[2,64,512]{2,1,0:T(8,128)(2,1)S(1)} %get-tuple-element.305), channel_id=1, source_target_pairs={{0,32},{8,40},{16,48},{24,56},{32,0},{40,8},{48,16},{56,24},{64,96... | collective-permute-start | bytes 393224 | tf_op jit(solution)/shard_map/ppermute | solution.py:21
  446.6 9.4 %collective-permute-start.118 = (bf16[2,64,1024]{2,1,0:T(8,128)(2,1)S(1)}, bf16[2,64,1024]{2,1,0:T(8,128)(2,1)S(1)}, u32[]{:S(2)}, u32[]{:S(2)}) collective-permute-start(bf16[2,64,1024]{2,1,0:T(8,128)(2,1)S(1)} %copy-done.93), channel_id=1, source_target_pairs={{0,32},{8,40},{16,48},{24,56},{32,0},{40,8},{48,16},{56,24},{64,96... | collective-permute-start | bytes 786440 | tf_op jit(solution)/shard_map/ppermute | solution.py:21
  450.6 8.6 %collective-permute-start.116 = (bf16[64,512]{1,0:T(8,128)(2,1)S(1)}, bf16[64,512]{1,0:T(8,128)(2,1)S(1)}, u32[]{:S(2)}, u32[]{:S(2)}) collective-permute-start(bf16[64,512]{1,0:T(8,128)(2,1)S(1)} %fusion.14), channel_id=1, source_target_pairs={{0,64},{8,72},{16,80},{24,88},{32,96},{40,104},{48,112},{56,120},{... | collective-permute-start | bytes 196616 | tf_op jit(solution)/shard_map/ppermute | solution.py:21
  (185 other events, 1334.9 us)
Sparse Core Ops, SparseCore 0:
  10.5 54.4 all-gather.3
  68.0 43.6 all-gather.5
  114.2 46.2 all-gather.7
  278.4 67.7 reduce-scatter.2
  350.4 70.1 reduce-scatter.4
